TPU v7x, 32 devices: a whole 2x2x4 slice. The times are simulated.
32 devices in a mesh: row: 4 (over x, core), col: 8 (over z, y).
Axes of the slice: x: 2, y: 2, z: 4, core: 2. Of those that a mesh axis runs over, the one named last changes fastest.
Arguments:
- activations: bfloat16 [64, 9216], P('row', 'col'), may hold values from -0.75 to 0.75
- cotangent: bfloat16 [64, 9216], P('col', 'row'), may hold values from -6 to 6
- weight: bfloat16 [9216, 9216], P('row', 'col'), may hold values from -0.0625 to 0.0625
- momentum: float32 [9216, 9216], P('row', 'col'), may hold values from -500 to 500
- right_factor: float32 [9216, 256], P('col'), may hold values from -6 to 6
Outputs:
- input_grad: bfloat16 [64, 9216], P('row', 'col')
- momentum_next: float32 [9216, 9216], P('row', 'col')
- right_next: float32 [9216, 256], P('col')
- weight_step: bfloat16 [9216, 9216], P('row', 'col')
All inputs are finite; a program needn't handle non-finite values.
Results may differ from a plain program's by a relative error of at most 0.0011.
Values may be sent and summed in bfloat16 or wider, within the bound.
A program may use at most 128 MiB of HBM per device.

v0:
```python
import functools

import jax
import jax.numpy as jnp
from jax import lax
from jax.experimental import pallas as pl
from jax.experimental.pallas import tpu as pltpu
from jax.sharding import PartitionSpec as P

momentum_decay = 0.6
ridge_weight = 0.001

HIGHEST = lax.Precision.HIGHEST
HIGH = lax.Precision.HIGH
SUBLANES = 8


def contract(left_side, right_side, left_dim, right_dim, precision):
    return lax.dot_general(
        left_side,
        right_side,
        (((left_dim,), (right_dim,)), ((), ())),
        precision=precision,
        preferred_element_type=jnp.float32,
    )


def identity(size):
    shape = (size, size)
    same = lax.broadcasted_iota(jnp.int32, shape, 0) == lax.broadcasted_iota(jnp.int32, shape, 1)
    return jnp.where(same, 1.0, 0.0).astype(jnp.float32)


def inverse_factor_kernel(block, ridge, gram_ref, inverse_ref, work, corner):
    size = gram_ref.shape[0]
    work[:, :size] = gram_ref[...] + ridge * identity(size)
    work[:, size:] = identity(size)
    row_in_group = lax.broadcasted_iota(jnp.int32, (SUBLANES, 2 * block), 0)
    for low in range(0, size, block):
        high = low + block
        corner[:, :block] = work[low:high, low:high]
        corner[:, block:] = identity(block)
        groups = [corner[g : g + SUBLANES, :] for g in range(0, block, SUBLANES)]
        for k in range(block):
            own, inside = divmod(k, SUBLANES)
            pivot_row = groups[own][inside : inside + 1, :]
            scaled = pivot_row / pivot_row[:, k : k + 1]
            for g in range(own, len(groups)):
                factor = groups[g][:, k : k + 1]
                change = factor * scaled
                if g == own:
                    change = jnp.where(row_in_group > inside, change, 0.0)
                groups[g] = groups[g] - change
        for g, rows in enumerate(groups):
            corner[g * SUBLANES : (g + 1) * SUBLANES, :] = rows
        pivots = jnp.sum(corner[:, :block] * identity(block), axis=1, keepdims=True)
        corner_inverse = corner[:, block:] * (1.0 / jnp.sqrt(pivots))
        panel = contract(corner_inverse, work[low:high, :], 1, 0, HIGHEST)
        inverse_ref[low:high, :] = panel[:, size:]
        if high < size:
            update = contract(panel[:, :size], panel, 0, 0, HIGHEST)
            work[high:, :] = work[high:, :] - update[high:, :]


def inverse_factor(gram_matrix, ridge):
    size = gram_matrix.shape[0]
    block = min(64, size)
    return pl.pallas_call(
        functools.partial(inverse_factor_kernel, block, ridge),
        out_shape=jax.ShapeDtypeStruct((size, size), jnp.float32),
        in_specs=[pl.BlockSpec(memory_space=pltpu.VMEM)],
        out_specs=pl.BlockSpec(memory_space=pltpu.VMEM),
        scratch_shapes=[
            pltpu.VMEM((size, 2 * size), jnp.float32),
            pltpu.VMEM((block, 2 * block), jnp.float32),
        ],
        cost_estimate=pl.CostEstimate(flops=20_000_000_000, bytes_accessed=8 * size * size, transcendentals=0),
        name="inverse_factor",
    )(gram_matrix)


def shards(rows_of, cols_of, activations, cotangent, weight, momentum, right_factor):
    dout = momentum.shape[0] * rows_of
    din = momentum.shape[1] * cols_of
    rank = right_factor.shape[1]
    cot_tokens = lax.all_gather(cotangent, "col", axis=0, tiled=True)
    act_tokens = lax.all_gather(activations, "row", axis=0, tiled=True)
    held_part = contract(momentum, right_factor, 1, 0, HIGH)
    act_part = contract(act_tokens.astype(jnp.float32), right_factor, 1, 0, HIGH)
    grad_part = contract(cot_tokens.astype(jnp.float32), act_part, 0, 0, HIGH)
    left_part = (held_part + grad_part) / jnp.sqrt(jnp.float32(din))
    left_piece = lax.psum_scatter(left_part, "col", scatter_dimension=0, tiled=True)
    input_part = jnp.dot(cot_tokens, weight, preferred_element_type=jnp.float32)
    buffer = momentum + contract(cot_tokens, act_tokens, 0, 0, None)
    left_block = lax.all_gather(left_piece, "col", axis=0, tiled=True)
    gram_matrix = lax.psum(contract(left_block, left_block, 0, 0, HIGHEST), "row")
    projected_part = contract(buffer, left_block, 0, 0, HIGH)
    gram_matrix, projected_part = lax.optimization_barrier((gram_matrix, projected_part))
    projected = lax.psum(projected_part, "row")
    projected, input_part = lax.optimization_barrier((projected, input_part))
    input_sums = lax.psum_scatter(input_part, "row", scatter_dimension=0, tiled=True)
    inverse = inverse_factor(gram_matrix, ridge_weight * dout)
    orthonormal = contract(left_block, inverse, 1, 1, HIGHEST)
    right = contract(projected, inverse, 1, 1, HIGHEST)
    squares = lax.psum(jnp.sum(right * right, axis=0), "col")
    momentum_next = buffer - (1.0 - momentum_decay) * contract(orthonormal, right, 1, 1, HIGH)
    right_next = right * lax.rsqrt(squares / din + 1e-06)
    step_scale = jnp.sqrt(jnp.float32(dout) / rank)
    weight_step = (step_scale * contract(orthonormal, right_next, 1, 1, HIGH)).astype(jnp.bfloat16)
    return (input_sums.astype(jnp.bfloat16), momentum_next, right_next, weight_step)


def solution(mesh):
    placed = (P("row", "col"), P("col", "row"), P("row", "col"), P("row", "col"), P("col", None))
    return jax.shard_map(
        functools.partial(shards, mesh.shape["row"], mesh.shape["col"]),
        mesh=mesh,
        in_specs=placed,
        out_specs=(P("row", "col"), P("row", "col"), P("col", None), P("row", "col")),
        check_vma=False,
    )
```

profile of v0, /device:TPU:0, one launch (start us, length us, event | category | flops | bytes accessed | tf_op | source)
XLA Modules:
  0.0 310.1 jit_solution(13287744790165177969)
XLA Ops:
  7.2 6.9 %all_gather.9 = bf16[64,1152]{1,0:T(8,128)(2,1)S(1)} all-gather(bf16[16,1152]{1,0:T(8,128)(2,1)} %param.5), channel_id=1, replica_groups=mesh['row'=4,'col'=8] {'row'}, dimensions={0}, use_global_device_ids=true | all-gather | bytes 184320 | tf_op jit(solution)/shard_map/all_gather | solution.py:87
  14.2 31.8 %all_gather.10 = bf16[64,2304]{1,0:T(8,128)(2,1)S(1)} all-gather(bf16[8,2304]{1,0:T(8,128)(2,1)} %param.6), channel_id=1, replica_groups=mesh['row'=4,'col'=8] {'col'}, dimensions={0}, use_global_device_ids=true | all-gather | bytes 331776 | tf_op jit(solution)/shard_map/all_gather | solution.py:86
  46.0 0.3 fusion.5
  46.3 7.6 %fusion.4 = f32[2304,256]{1,0:T(8,128)S(1)} fusion(f32[2304,1152]{1,0:T(8,128)} %param.8, f32[1152,256]{1,0:T(8,128)S(1)} %copy-done), kind=kOutput, calls=%fused_computation.11 | convolution fusion | flops 4076863488 | bytes 14155776 | tf_op jit(solution)/shard_map/dot_general | solution.py:19
  53.9 2.2 fusion.3
  56.2 0.0 all-gather.2.cloned.1.call-start
  56.2 70.6 %reduce-scatter.3.cloned.1.call-done = f32[288,256]{1,0:T(8,128)} async-done(((f32[2304,256]{1,0:T(8,128)}), f32[288,256]{1,0:T(8,128)}) %reduce-scatter.3.cloned.1.call-update) | async-done | bytes 294928 | tf_op jit(solution)/shard_map/reduce_scatter | solution.py:92
  126.9 4.3 %fusion.8 = f32[64,1152]{1,0:T(8,128)} fusion(bf16[64,2304]{1,0:T(8,128)(2,1)S(1)} %all_gather.10, bf16[2304,1152]{1,0:T(8,128)(2,1)} %param.7), kind=kOutput, calls=%fused_computation.15 | convolution fusion | flops 339738624 | bytes 5898240 | tf_op jit(solution)/shard_map/dot_general | solution.py:93
  131.2 9.7 %convolution_add_fusion = f32[2304,1152]{1,0:T(8,128)} fusion(f32[2304,1152]{1,0:T(8,128)} %param.8, bf16[64,2304]{1,0:T(8,128)(2,1)S(1)} %all_gather.10, bf16[64,1152]{1,0:T(8,128)(2,1)S(1)} %all_gather.9), kind=kOutput, calls=%fused_computation.3 | convolution fusion | flops 342392832 | bytes 21676032 | tf_op jit(solution)/shard_map/dot_general | solution.py:19
  140.9 39.2 %all-gather.2.cloned.1.call-done = f32[2304,256]{1,0:T(8,128)} async-done(((f32[288,256]{1,0:T(8,128)}), f32[2304,256]{1,0:T(8,128)}) %all-gather.2.cloned.1.call-update) | async-done | bytes 2359312 | tf_op jit(solution)/shard_map/all_gather | solution.py:95
  180.1 7.1 %fusion.6 = f32[256,256]{1,0:T(8,128)} fusion(f32[2304,256]{1,0:T(8,128)} %all-gather.2.cloned.1.call-done), kind=kOutput, calls=%fused_computation.13 | convolution fusion | flops 1811939328 | bytes 2621440 | tf_op jit(solution)/shard_map/dot_general | solution.py:19
  187.2 0.2 all-reduce.5.cloned.1.call-start
  187.4 12.2 %fusion.7 = f32[1152,256]{1,0:T(8,128)} fusion(f32[2304,1152]{1,0:T(8,128)} %convolution_add_fusion, f32[2304,256]{1,0:T(8,128)S(1)} %copy-done.1), kind=kOutput, calls=%fused_computation.14 | convolution fusion | flops 4076863488 | bytes 14155776 | tf_op jit(solution)/shard_map/dot_general | solution.py:19
  199.7 18.5 %all-reduce.3.cloned.1.call-done.gram_ref = f32[256,256]{1,0:T(8,128)} async-done(((f32[256,256]{1,0:T(8,128)}), f32[256,256]{1,0:T(8,128)}) %all-reduce.3.cloned.1.call-update) | async-done | bytes 262160 | tf_op jit(solution)/shard_map/psum | solution.py:96
  218.2 26.2 %inverse_factor.1 = f32[256,256]{1,0:T(8,128)} custom-call(f32[256,256]{1,0:T(8,128)} %all-reduce.3.cloned.1.call-done.gram_ref), custom_call_target="tpu_custom_call" | custom-call | flops 20000000000 | bytes 524288 | tf_op jit(solution)/shard_map/inverse_factor/pallas_call | solution.py:68
  244.5 4.4 %fusion.9 = f32[2304,256]{1,0:T(8,128)} fusion(f32[2304,256]{1,0:T(8,128)S(1)} %copy-done.1, f32[256,256]{1,0:T(8,128)} %inverse_factor.1), kind=kOutput, calls=%fused_computation.16 | convolution fusion | flops 1811939328 | bytes 4980736 | tf_op jit(solution)/shard_map/dot_general | solution.py:19
  248.9 9.9 %all-reduce.5.cloned.1.call-done = f32[1152,256]{1,0:T(8,128)} async-done(((f32[1152,256]{1,0:T(8,128)}), f32[1152,256]{1,0:T(8,128)}) %all-reduce.5.cloned.1.call-update) | async-done | bytes 1179664 | tf_op jit(solution)/shard_map/psum | solution.py:99
  258.8 3.4 %multiply_reduce_fusion = (f32[256]{0:T(256)S(1)}, f32[1152,256]{1,0:T(8,128)}) fusion(f32[1152,256]{1,0:T(8,128)} %all-reduce.5.cloned.1.call-done, f32[256,256]{1,0:T(8,128)} %inverse_factor.1), kind=kOutput, calls=%fused_computation.8 | convolution fusion | flops 906559232 | bytes 2622464 | tf_op jit(solution)/shard_map/dot_general | solution.py:19
  262.2 21.6 %psum.23 = f32[256]{0:T(256)S(1)} all-reduce(f32[256]{0:T(256)S(1)} %get-tuple-element.12), channel_id=1, replica_groups=mesh['row'=4,'col'=8] {'col'}, use_global_device_ids=true, to_apply=%region_5.0 | all-reduce | flops 256 | bytes 2048 | tf_op jit(solution)/shard_map/psum | solution.py:105
  283.8 10.5 %fusion = f32[2304,1152]{1,0:T(8,128)} fusion(f32[2304,1152]{1,0:T(8,128)} %convolution_add_fusion, f32[2304,256]{1,0:T(8,128)S(1)} %copy-done.2, f32[1152,256]{1,0:T(8,128)} %get-tuple-element.13), kind=kOutput, calls=%fused_computation.2 | convolution fusion | flops 4082171904 | bytes 24772608 | tf_op jit(solution)/shard_map/dot_general | solution.py:19
  294.3 0.1 broadcast_multiply_fusion
  294.4 1.0 copy-done.4
  295.4 6.7 %fusion.1 = bf16[2304,1152]{1,0:T(8,128)(2,1)} fusion(f32[2304,256]{1,0:T(8,128)S(1)} %copy-done.2, f32[1152,256]{1,0:T(8,128)S(1)} %broadcast_multiply_fusion), kind=kOutput, calls=%fused_computation.4 | convolution fusion | flops 4082171904 | bytes 8847360 | tf_op jit(solution)/shard_map/dot_general | solution.py:19
  302.0 1.5 convert_element_type.8
  (19 shorter events, 0.2 us)
Async XLA Ops:
  7.2 38.8 %copy-start = (f32[1152,256]{1,0:T(8,128)S(1)}, f32[1152,256]{1,0:T(8,128)}, u32[]{:S(2)}) copy-start(f32[1152,256]{1,0:T(8,128)} %param.9) | copy-start | bytes 3538948
  7.2 119.6 %reduce-scatter.3.cloned.1.call-start = ((), (), s32[]{:S(2)}) async-start(), calls=%async_computation.2 | async-start | bytes 2654208 | tf_op jit(solution)/shard_map/reduce_scatter | solution.py:92
  56.2 123.9 %all-gather.2.cloned.1.call-start = ((), (), s32[]{:S(2)}) async-start(), calls=%async_computation.3 | async-start | bytes 2654208 | tf_op jit(solution)/shard_map/all_gather | solution.py:95
  126.8 91.3 %all-reduce.3.cloned.1.call-start = ((), (), s32[]{:S(2)}) async-start(), calls=%async_computation.4 | async-start | bytes 524288 | tf_op jit(solution)/shard_map/psum | solution.py:96
  180.1 7.4 %copy-start.1 = (f32[2304,256]{1,0:T(8,128)S(1)}, f32[2304,256]{1,0:T(8,128)}, u32[]{:S(2)}) copy-start(f32[2304,256]{1,0:T(8,128)} %all-gather.2.cloned.1.call-done) | copy-start | bytes 7077892
  187.2 71.5 %all-reduce.5.cloned.1.call-start = ((), (), s32[]{:S(2)}) async-start(), calls=%async_computation.5 | async-start | bytes 2359296 | tf_op jit(solution)/shard_map/psum | solution.py:99
  218.2 83.9 %reduce-scatter.5.cloned.1.call-start = ((), (), s32[]{:S(2)}) async-start(), calls=%async_computation.6 | async-start | bytes 368640 | tf_op jit(solution)/shard_map/reduce_scatter | solution.py:101
  248.9 34.9 %copy-start.2 = (f32[2304,256]{1,0:T(8,128)S(1)}, f32[2304,256]{1,0:T(8,128)}, u32[]{:S(2)}) copy-start(f32[2304,256]{1,0:T(8,128)} %fusion.9) | copy-start | bytes 7077892
  283.8 10.5 %copy-start.3 = (f32[1152,256]{1,0:T(8,128)S(1)}, f32[1152,256]{1,0:T(8,128)}, u32[]{:S(2)}) copy-start(f32[1152,256]{1,0:T(8,128)} %get-tuple-element.13) | copy-start | bytes 3538948
  294.4 1.0 copy-start.4
Sparse Core Ops, SparseCore 0:
  56.3 70.4 reduce-scatter.2
  129.0 51.0 all-gather.1
  187.3 30.8 all-reduce.2
  221.0 37.7 all-reduce.4
  261.1 20.3 reduce-scatter.4
where the time goes:
time: 310 us
  waiting for transfers between devices  138 us (45%)
  matrix products  68.4 us (22%)
  blocking collectives  60.3 us (19%)
  Pallas kernels  26.2 us (8%)
  between operations  13.8 us (4%)
    reduce_scatter x1, waiting for transfers between devices, shards(): lax.psum_scatter(left_part, 'col', scatter_dimension=0, tiled=True)  70.6 us
    dot_general x10, matrix products, contract(): lax.dot_general(left_side, right_side, (((left_dim,), (right_dim,)), ((),...  64.2 us
    all_gather x1, waiting for transfers between devices, shards(): left_block = lax.all_gather(left_piece, 'col', axis=0, tiled=True)  39.2 us
    all_gather x1, blocking collectives, shards(): cot_tokens = lax.all_gather(cotangent, 'col', axis=0, tiled=True)  31.8 us
    pallas_call x1, Pallas kernels, inverse_factor(): pl.pallas_call(functools.partial(inverse_factor_kernel, block, ridge), ou...  26.2 us
    psum x1, blocking collectives, shards(): squares = lax.psum(jnp.sum(right * right, axis=0), 'col')  21.6 us
    psum x1, waiting for transfers between devices, shards(): lax.psum(contract(left_block, left_block, 0, 0, HIGHEST), 'row')  18.5 us
    psum x1, waiting for transfers between devices, shards(): projected = lax.psum(projected_part, 'row')  9.88 us
  transfers between devices with their start and end apart: 5, of which 4 were waited for; matrix products, arithmetic and copies ran while one was open for 17% of the time, Pallas kernels for 8%

commit v1 on v0

--- a/solution.py
+++ b/solution.py
@@ -13,9 +13,11 @@
 HIGHEST = lax.Precision.HIGHEST
 HIGH = lax.Precision.HIGH
 SUBLANES = 8
-
-
-def contract(left_side, right_side, left_dim, right_dim, precision):
+LANES = 128
+MESH = pl.DeviceIdType.MESH
+
+
+def contract(left_side, right_side, left_dim, right_dim, precision=None):
     return lax.dot_general(
         left_side,
         right_side,
@@ -31,7 +33,23 @@
     return jnp.where(same, 1.0, 0.0).astype(jnp.float32)
 
 
-def inverse_factor_kernel(block, ridge, gram_ref, inverse_ref, work, corner):
+def two_stages(size):
+    inner = max(k for k in range(1, size + 1) if size % k == 0 and k * k <= size)
+    return inner, size // inner
+
+
+def split(value):
+    high = value.astype(jnp.bfloat16)
+    return high, (value - high.astype(jnp.float32)).astype(jnp.bfloat16)
+
+
+def contract_split(left_pair, right_pair, left_dim, right_dim):
+    total = contract(left_pair[0], right_pair[0], left_dim, right_dim)
+    total = total + contract(left_pair[1], right_pair[0], left_dim, right_dim)
+    return total + contract(left_pair[0], right_pair[1], left_dim, right_dim)
+
+
+def inverse_factor_body(block, ridge, gram_ref, inverse_ref, work, corner):
     size = gram_ref.shape[0]
     work[:, :size] = gram_ref[...] + ridge * identity(size)
     work[:, size:] = identity(size)
@@ -66,7 +84,7 @@
     size = gram_matrix.shape[0]
     block = min(64, size)
     return pl.pallas_call(
-        functools.partial(inverse_factor_kernel, block, ridge),
+        functools.partial(inverse_factor_body, block, ridge),
         out_shape=jax.ShapeDtypeStruct((size, size), jnp.float32),
         in_specs=[pl.BlockSpec(memory_space=pltpu.VMEM)],
         out_specs=pl.BlockSpec(memory_space=pltpu.VMEM),
@@ -79,7 +97,7 @@
     )(gram_matrix)
 
 
-def shards(rows_of, cols_of, activations, cotangent, weight, momentum, right_factor):
+def plain_shards(rows_of, cols_of, activations, cotangent, weight, momentum, right_factor):
     dout = momentum.shape[0] * rows_of
     din = momentum.shape[1] * cols_of
     rank = right_factor.shape[1]
@@ -110,6 +128,559 @@
     return (input_sums.astype(jnp.bfloat16), momentum_next, right_next, weight_step)
 
 
+def remote(source, target, send_sem, recv_sem, device):
+    return pltpu.make_async_remote_copy(
+        src_ref=source,
+        dst_ref=target,
+        send_sem=send_sem,
+        recv_sem=recv_sem,
+        device_id=device,
+        device_id_type=MESH,
+    )
+
+
+def greet(devices):
+    barrier = pltpu.get_barrier_semaphore()
+    for device in devices:
+        pl.semaphore_signal(barrier, inc=1, device_id=device, device_id_type=MESH)
+    pl.semaphore_wait(barrier, len(devices))
+
+
+def left_kernel(
+    n_row,
+    n_col,
+    act_ref,
+    cot_ref,
+    weight_hbm,
+    momentum_hbm,
+    factor_ref,
+    left_ref,
+    projected_ref,
+    gram_ref,
+    input_ref,
+    buffer_hbm,
+    act_all,
+    cot_all,
+    cot_flat,
+    cot_turned,
+    chunks,
+    chunk_high,
+    chunk_low,
+    weight,
+    factor_high,
+    factor_low,
+    send_inner,
+    recv_inner,
+    totals,
+    recv_outer,
+    input_send,
+    input_recv,
+    load_sem,
+    store_sem,
+    weight_sem,
+    act_sem,
+    cot_sem,
+    inner_sem,
+    outer_sem,
+    gather_outer_sem,
+    gather_inner_sem,
+    input_sem,
+):
+    inner, outer = two_stages(n_col)
+    row, col = lax.axis_index("row"), lax.axis_index("col")
+    me_in, me_out = lax.rem(col, inner), lax.div(col, inner)
+    piece, cols = chunks.shape[1], chunks.shape[2]
+    din = cols * n_col
+    act_rows = act_ref.shape[0]
+    tokens = act_rows * n_row
+
+    def outer_id(k):
+        return lax.rem(me_out + 1 + k, outer)
+
+    def chunk_at(j):
+        d, k = divmod(j, outer) if isinstance(j, int) else (lax.div(j, outer), lax.rem(j, outer))
+        return outer_id(k) * inner + lax.rem(me_in + 1 + d, inner)
+
+    def load(j):
+        q = chunk_at(j)
+        return pltpu.make_async_copy(
+            momentum_hbm.at[pl.ds(pl.multiple_of(q * piece, SUBLANES), piece), :], chunks.at[j], load_sem.at[j]
+        )
+
+    def store(j):
+        q = chunk_at(j)
+        return pltpu.make_async_copy(
+            chunks.at[j], buffer_hbm.at[pl.ds(pl.multiple_of(q * piece, SUBLANES), piece), :], store_sem.at[j]
+        )
+
+    for j in range(n_col):
+        load(j).start()
+    weight_copy = pltpu.make_async_copy(weight_hbm, weight, weight_sem)
+    weight_copy.start()
+
+    row_peers = [lax.rem(row + d, n_row) for d in range(1, n_row)]
+    col_peers = [lax.rem(col + d, n_col) for d in range(1, n_col)]
+    greet([(peer, col) for peer in row_peers] + [(row, peer) for peer in col_peers])
+
+    cot_copies = [
+        remote(cot_ref, cot_all.at[col], cot_sem.at[0, d], cot_sem.at[1, d], (row, peer))
+        for d, peer in enumerate(col_peers)
+    ]
+    act_copies = [
+        remote(act_ref, act_all.at[row], act_sem.at[0, d], act_sem.at[1, d], (peer, col))
+        for d, peer in enumerate(row_peers)
+    ]
+    for copy in cot_copies + act_copies:
+        copy.start()
+    act_all[row] = act_ref[...]
+    cot_all[col] = cot_ref[...]
+    factor_high[...], factor_low[...] = split(factor_ref[...])
+    for copy in act_copies + cot_copies:
+        copy.wait()
+
+    def turn(b, carry):
+        lanes = pl.ds(pl.multiple_of(b * LANES, LANES), LANES)
+        slab = cot_all[:, :, lanes].astype(jnp.float32).reshape(tokens, LANES)
+        cot_flat[:, lanes] = slab.astype(jnp.bfloat16)
+        cot_turned[lanes, :] = slab.T.astype(jnp.bfloat16)
+        return carry
+
+    lax.fori_loop(0, cot_ref.shape[1] // LANES, turn, 0)
+
+    def partial(j):
+        q = chunk_at(j)
+        load(j).wait()
+        turned = cot_turned[pl.ds(pl.multiple_of(q * piece, 2 * SUBLANES), piece), :]
+        value = chunks[j] + contract(turned, act_all[...].reshape(tokens, cols), 1, 0)
+        chunks[j] = value
+        high, low = split(value)
+        chunk_high[j] = high
+        chunk_low[j] = low
+        return contract_split((high, low), (factor_high[...], factor_low[...]), 1, 0)
+
+    def inner_copy(d, k):
+        peer = me_out * inner + lax.rem(me_in + 1 + d, inner)
+        return remote(
+            send_inner.at[d, k], recv_inner.at[d, k], inner_sem.at[0, d, k], inner_sem.at[1, d, k], (row, peer)
+        )
+
+    def outer_copy(k):
+        peer = outer_id(k) * inner + me_in
+        return remote(totals.at[k], recv_outer.at[k], outer_sem.at[0, k], outer_sem.at[1, k], (row, peer))
+
+    for d in range(inner - 1):
+
+        def push(k, carry, d=d):
+            send_inner[d, k] = partial(d * outer + k)
+            inner_copy(d, k).start()
+            return carry
+
+        lax.fori_loop(0, outer, push, 0)
+
+    def keep(k, carry):
+        totals[k] = partial((inner - 1) * outer + k)
+        return carry
+
+    lax.fori_loop(0, outer, keep, 0)
+
+    for j in range(n_col):
+        store(j).start()
+
+    weight_copy.wait()
+    input_part = contract(cot_flat[...], weight[...], 1, 0)
+    input_send[...] = input_part.reshape(n_row, act_rows, cols)
+    input_copies = [
+        remote(input_send.at[peer], input_recv.at[d], input_sem.at[0, d], input_sem.at[1, d], (peer, col))
+        for d, peer in enumerate(row_peers)
+    ]
+    for copy in input_copies:
+        copy.start()
+
+    for k in range(outer):
+        total = totals[k]
+        for d in range(inner - 1):
+            inner_copy(d, k).wait()
+            total = total + recv_inner[d, k]
+        totals[k] = total
+        if k < outer - 1:
+            outer_copy(k).start()
+    mine = totals[outer - 1]
+    for k in range(outer - 1):
+        outer_copy(k).wait()
+        mine = mine + recv_outer[k]
+    left_ref[col] = mine / jnp.sqrt(jnp.float32(din))
+
+    def gather_outer(k):
+        peer = outer_id(k) * inner + me_in
+        return remote(
+            left_ref.at[col], left_ref.at[col], gather_outer_sem.at[0, k], gather_outer_sem.at[1, k], (row, peer)
+        )
+
+    def source_outer(k):
+        return lax.rem(me_out + outer - k, outer)
+
+    def gather_inner(d, k):
+        q = source_outer(k) * inner + me_in
+        peer = me_out * inner + lax.rem(me_in + 1 + d, inner)
+        return remote(
+            left_ref.at[q], left_ref.at[q], gather_inner_sem.at[0, d, k], gather_inner_sem.at[1, d, k], (row, peer)
+        )
+
+    for k in range(outer - 1):
+        gather_outer(k).start()
+    for d in range(inner - 1):
+        gather_inner(d, 0).start()
+
+    def place(q):
+        d = lax.rem(lax.rem(q, inner) - me_in - 1 + 2 * inner, inner)
+        k = lax.rem(lax.div(q, inner) - me_out - 1 + 2 * outer, outer)
+        return d * outer + k
+
+    def absorb(q, first):
+        value = left_ref[q]
+        pair = split(value)
+        j = place(q)
+        gram = contract(value, value, 0, 0, HIGHEST)
+        projected = contract_split(pair, (chunk_high[j], chunk_low[j]), 0, 0)
+        if first:
+            gram_ref[...] = gram
+            projected_ref[...] = projected
+        else:
+            gram_ref[...] = gram_ref[...] + gram
+            projected_ref[...] = projected_ref[...] + projected
+
+    absorb(col, True)
+    for k in range(1, outer):
+        gather_outer(k - 1).wait()
+        for d in range(inner - 1):
+            gather_inner(d, k).start()
+        absorb(source_outer(k) * inner + me_in, False)
+        for d in range(inner - 1):
+            gather_inner(d, k - 1).wait()
+            absorb(source_outer(k - 1) * inner + lax.rem(me_in - 1 - d + inner, inner), False)
+    for d in range(inner - 1):
+        gather_inner(d, outer - 1).wait()
+        absorb(source_outer(outer - 1) * inner + lax.rem(me_in - 1 - d + inner, inner), False)
+
+    total = input_send[row]
+    for d, copy in enumerate(input_copies):
+        copy.wait()
+        total = total + input_recv[d]
+    input_ref[...] = total.astype(jnp.bfloat16)
+    for j in range(n_col):
+        store(j).wait()
+
+
+def left_call(n_row, n_col, activations, cotangent, weight, momentum, right_factor):
+    inner, outer = two_stages(n_col)
+    rows, cols = momentum.shape
+    rank = right_factor.shape[1]
+    piece = rows // n_col
+    act_rows, cot_rows = activations.shape[0], cotangent.shape[0]
+    tokens = act_rows * n_row
+    f32, bf16 = jnp.float32, jnp.bfloat16
+    vmem = pl.BlockSpec(memory_space=pltpu.VMEM)
+    hbm = pl.BlockSpec(memory_space=pl.ANY)
+    dma = pltpu.SemaphoreType.DMA
+    return pl.pallas_call(
+        functools.partial(left_kernel, n_row, n_col),
+        out_shape=(
+            jax.ShapeDtypeStruct((n_col, piece, rank), f32),
+            jax.ShapeDtypeStruct((rank, cols), f32),
+            jax.ShapeDtypeStruct((rank, rank), f32),
+            jax.ShapeDtypeStruct((act_rows, cols), bf16),
+            jax.ShapeDtypeStruct((rows, cols), f32),
+        ),
+        in_specs=[vmem, vmem, hbm, hbm, vmem],
+        out_specs=(vmem, vmem, vmem, vmem, hbm),
+        scratch_shapes=[
+            pltpu.VMEM((n_row, act_rows, cols), bf16),
+            pltpu.VMEM((n_col, cot_rows, rows), bf16),
+            pltpu.VMEM((tokens, rows), bf16),
+            pltpu.VMEM((rows, tokens), bf16),
+            pltpu.VMEM((n_col, piece, cols), f32),
+            pltpu.VMEM((n_col, piece, cols), bf16),
+            pltpu.VMEM((n_col, piece, cols), bf16),
+            pltpu.VMEM((rows, cols), bf16),
+            pltpu.VMEM((cols, rank), bf16),
+            pltpu.VMEM((cols, rank), bf16),
+            pltpu.VMEM((inner - 1, outer, piece, rank), f32),
+            pltpu.VMEM((inner - 1, outer, piece, rank), f32),
+            pltpu.VMEM((outer, piece, rank), f32),
+            pltpu.VMEM((outer - 1, piece, rank), f32),
+            pltpu.VMEM((n_row, act_rows, cols), f32),
+            pltpu.VMEM((n_row - 1, act_rows, cols), f32),
+            dma((n_col,)),
+            dma((n_col,)),
+            dma,
+            dma((2, n_row - 1)),
+            dma((2, n_col - 1)),
+            dma((2, inner - 1, outer)),
+            dma((2, outer - 1)),
+            dma((2, outer - 1)),
+            dma((2, inner - 1, outer)),
+            dma((2, n_row - 1)),
+        ],
+        compiler_params=pltpu.CompilerParams(
+            collective_id=1, has_side_effects=True, vmem_limit_bytes=60 * 1024 * 1024
+        ),
+        name="left_factor",
+    )(activations, cotangent, weight, momentum, right_factor)
+
+
+def right_kernel(
+    n_row,
+    n_col,
+    ridge,
+    din,
+    gram_ref,
+    projected_ref,
+    left_ref,
+    orthonormal_ref,
+    right_ref,
+    scale_ref,
+    gram_in,
+    gram_out,
+    gram_all,
+    proj_in,
+    proj_out,
+    proj_all,
+    inverse,
+    work,
+    corner,
+    squares_all,
+    gram_in_sem,
+    gram_out_sem,
+    gram_all_sem,
+    proj_in_sem,
+    proj_out_sem,
+    proj_all_sem,
+    squares_sem,
+):
+    inner, outer = two_stages(n_row)
+    row, col = lax.axis_index("row"), lax.axis_index("col")
+    me_in, me_out = lax.rem(row, inner), lax.div(row, inner)
+    rank = gram_ref.shape[0]
+    part = rank // inner
+    inner_peers = [(lax.rem(me_in + 1 + d, inner)) for d in range(inner - 1)]
+    outer_peers = [(lax.rem(me_out + 1 + d, outer)) for d in range(outer - 1)]
+    col_peers = [lax.rem(col + d, n_col) for d in range(1, n_col)]
+    greet(
+        [(me_out * inner + peer, col) for peer in inner_peers]
+        + [(peer * inner + me_in, col) for peer in outer_peers]
+        + [(row, peer) for peer in col_peers]
+    )
+
+    def at(index):
+        return pl.ds(pl.multiple_of(index * part, SUBLANES), part)
+
+    def reduce_in(source, buffer, sem):
+        copies = [
+            remote(source.at[at(peer), :], buffer.at[d], sem.at[0, d], sem.at[1, d], (me_out * inner + peer, col))
+            for d, peer in enumerate(inner_peers)
+        ]
+        for copy in copies:
+            copy.start()
+        return copies
+
+    def exchange_out(source, copies_in, buffer_in, buffer_out, sem):
+        total = source[at(me_in), :]
+        for d, copy in enumerate(copies_in):
+            copy.wait()
+            total = total + buffer_in[d]
+        buffer_out[me_out] = total
+        copies = [
+            remote(
+                buffer_out.at[me_out], buffer_out.at[me_out], sem.at[0, d], sem.at[1, d], (peer * inner + me_in, col)
+            )
+            for d, peer in enumerate(outer_peers)
+        ]
+        for copy in copies:
+            copy.start()
+        return copies
+
+    def gather_in(copies_out, buffer_out, whole, sem):
+        for copy in copies_out:
+            copy.wait()
+        total = buffer_out[0]
+        for o in range(1, outer):
+            total = total + buffer_out[o]
+        whole[at(me_in), :] = total
+        copies = [
+            remote(
+                whole.at[at(me_in), :], whole.at[at(me_in), :], sem.at[0, d], sem.at[1, d], (me_out * inner + peer, col)
+            )
+            for d, peer in enumerate(inner_peers)
+        ]
+        for copy in copies:
+            copy.start()
+        return copies
+
+    gram_copies = reduce_in(gram_ref, gram_in, gram_in_sem)
+    proj_copies = reduce_in(projected_ref, proj_in, proj_in_sem)
+    gram_copies = exchange_out(gram_ref, gram_copies, gram_in, gram_out, gram_out_sem)
+    proj_copies = exchange_out(projected_ref, proj_copies, proj_in, proj_out, proj_out_sem)
+    gram_copies = gather_in(gram_copies, gram_out, gram_all, gram_all_sem)
+    for copy in gram_copies:
+        copy.wait()
+    inverse_factor_body(corner.shape[0], ridge, gram_all, inverse, work, corner)
+    proj_copies = gather_in(proj_copies, proj_out, proj_all, proj_all_sem)
+    factor = split(inverse[...])
+    for q in range(n_col):
+        orthonormal_ref[q] = contract_split(split(left_ref[q]), factor, 1, 1)
+    for copy in proj_copies:
+        copy.wait()
+    right = contract_split(factor, split(proj_all[...]), 1, 0)
+    right_ref[...] = right
+    squares = jnp.sum(right * right, axis=1, keepdims=True)
+    squares = jnp.broadcast_to(squares, (rank, LANES)).T[:SUBLANES, :]
+    squares_all[col] = squares
+    copies = [
+        remote(squares_all.at[col], squares_all.at[col], squares_sem.at[0, d], squares_sem.at[1, d], (row, peer))
+        for d, peer in enumerate(col_peers)
+    ]
+    for copy in copies:
+        copy.start()
+    for copy in copies:
+        copy.wait()
+    total = squares_all[0]
+    for q in range(1, n_col):
+        total = total + squares_all[q]
+    scale_ref[...] = lax.rsqrt(total / din + 1e-06)
+
+
+def right_call(n_row, n_col, ridge, din, gram_part, projected_part, left):
+    inner, outer = two_stages(n_row)
+    rank, cols = projected_part.shape
+    part = rank // inner
+    block = min(64, rank)
+    f32 = jnp.float32
+    vmem = pl.BlockSpec(memory_space=pltpu.VMEM)
+    dma = pltpu.SemaphoreType.DMA
+    return pl.pallas_call(
+        functools.partial(right_kernel, n_row, n_col, ridge, din),
+        out_shape=(
+            jax.ShapeDtypeStruct(left.shape, f32),
+            jax.ShapeDtypeStruct((rank, cols), f32),
+            jax.ShapeDtypeStruct((SUBLANES, rank), f32),
+        ),
+        in_specs=[vmem] * 3,
+        out_specs=(vmem,) * 3,
+        scratch_shapes=[
+            pltpu.VMEM((inner - 1, part, rank), f32),
+            pltpu.VMEM((outer, part, rank), f32),
+            pltpu.VMEM((rank, rank), f32),
+            pltpu.VMEM((inner - 1, part, cols), f32),
+            pltpu.VMEM((outer, part, cols), f32),
+            pltpu.VMEM((rank, cols), f32),
+            pltpu.VMEM((rank, rank), f32),
+            pltpu.VMEM((rank, 2 * rank), f32),
+            pltpu.VMEM((block, 2 * block), f32),
+            pltpu.VMEM((n_col, SUBLANES, rank), f32),
+            dma((2, inner - 1)),
+            dma((2, outer - 1)),
+            dma((2, inner - 1)),
+            dma((2, inner - 1)),
+            dma((2, outer - 1)),
+            dma((2, inner - 1)),
+            dma((2, n_col - 1)),
+        ],
+        compiler_params=pltpu.CompilerParams(
+            collective_id=2, has_side_effects=True, vmem_limit_bytes=60 * 1024 * 1024
+        ),
+        name="right_factor",
+    )(gram_part, projected_part, left)
+
+
+def output_kernel(
+    step_scale,
+    buffer_ref,
+    orthonormal_ref,
+    right_ref,
+    scale_ref,
+    momentum_ref,
+    step_ref,
+    next_ref,
+    right_high,
+    right_low,
+):
+    @pl.when(pl.program_id(0) == 0)
+    def _():
+        right_high[...], right_low[...] = split(right_ref[...])
+        next_ref[...] = right_ref[...].T * scale_ref[:1, :]
+
+    right = (right_high[...], right_low[...])
+    orthonormal = orthonormal_ref[...]
+    momentum_ref[...] = buffer_ref[...] - (1.0 - momentum_decay) * contract_split(split(orthonormal), right, 1, 0)
+    scaled = orthonormal * scale_ref[:1, :]
+    step_ref[...] = (step_scale * contract_split(split(scaled), right, 1, 0)).astype(jnp.bfloat16)
+
+
+def output_call(step_scale, buffer, orthonormal, right, scale):
+    rows, cols = buffer.shape
+    rank = right.shape[0]
+    tile = max(t for t in range(16, 289, 16) if rows % t == 0)
+    f32 = jnp.float32
+    return pl.pallas_call(
+        functools.partial(output_kernel, step_scale),
+        grid=(rows // tile,),
+        out_shape=(
+            jax.ShapeDtypeStruct((rows, cols), f32),
+            jax.ShapeDtypeStruct((rows, cols), jnp.bfloat16),
+            jax.ShapeDtypeStruct((cols, rank), f32),
+        ),
+        in_specs=[
+            pl.BlockSpec((tile, cols), lambda i: (i, 0)),
+            pl.BlockSpec((tile, rank), lambda i: (i, 0)),
+            pl.BlockSpec((rank, cols), lambda i: (0, 0)),
+            pl.BlockSpec(scale.shape, lambda i: (0, 0)),
+        ],
+        out_specs=(
+            pl.BlockSpec((tile, cols), lambda i: (i, 0)),
+            pl.BlockSpec((tile, cols), lambda i: (i, 0)),
+            pl.BlockSpec((cols, rank), lambda i: (0, 0)),
+        ),
+        scratch_shapes=[pltpu.VMEM((rank, cols), jnp.bfloat16), pltpu.VMEM((rank, cols), jnp.bfloat16)],
+        compiler_params=pltpu.CompilerParams(
+            dimension_semantics=("arbitrary",), vmem_limit_bytes=40 * 1024 * 1024
+        ),
+        name="outputs",
+    )(buffer, orthonormal, right, scale)
+
+
+def kernel_shards(n_row, n_col, activations, cotangent, weight, momentum, right_factor):
+    rows, cols = momentum.shape
+    rank = right_factor.shape[1]
+    dout, din = rows * n_row, cols * n_col
+    left, projected, gram, input_grad, buffer = left_call(
+        n_row, n_col, activations, cotangent, weight, momentum, right_factor
+    )
+    orthonormal, right, scale = right_call(n_row, n_col, ridge_weight * dout, din, gram, projected, left)
+    step_scale = (dout / rank) ** 0.5
+    momentum_next, weight_step, right_next = output_call(
+        step_scale, buffer, orthonormal.reshape(rows, rank), right, scale
+    )
+    return input_grad, momentum_next, right_next, weight_step
+
+
+def shards(n_row, n_col, activations, cotangent, weight, momentum, right_factor):
+    rows, cols = momentum.shape
+    rank = right_factor.shape[1]
+    aligned = (
+        rows % (n_col * 2 * SUBLANES) == 0
+        and rows % LANES == 0
+        and cols % LANES == 0
+        and rank % LANES == 0
+        and activations.shape[0] % (2 * SUBLANES) == 0
+        and cotangent.shape[0] % SUBLANES == 0
+        and two_stages(n_row)[0] > 1
+        and two_stages(n_col)[0] > 1
+        and rank % (two_stages(n_row)[0] * SUBLANES) == 0
+    )
+    chosen = kernel_shards if aligned else plain_shards
+    return chosen(n_row, n_col, activations, cotangent, weight, momentum, right_factor)
+
+
 def solution(mesh):
     placed = (P("row", "col"), P("col", "row"), P("row", "col"), P("row", "col"), P("col", None))
     return jax.shard_map(

time: 310 us -> 166 us (0.54)
  waiting for transfers between devices: 138 us -> 0 us
  Pallas kernels: 26.2 us -> 156 us
  matrix products: 68.4 us -> 0 us
  blocking collectives: 60.3 us -> 0 us
  between operations: 13.8 us -> 0.66 us
  local copies, waits for them, and re-layouts: 1.03 us -> 8.26 us
    pallas_call x1 -> x3, Pallas kernels: 26.2 us -> 156 us  [the longest x1 91.2 us: left_call(): pl.pallas_call(functools.partial(left_kernel, n_row, n_col), out_shape=(j...]
    reduce_scatter x2 -> x0, waiting for transfers between devices: 70.6 us -> none  [the longest x1 70.6 us: shards(): lax.psum_scatter(left_part, 'col', scatter_dimension=0, tiled=True)]
    dot_general x11 -> x0, matrix products: 68.4 us -> none  [the longest x10 64.2 us: contract(): lax.dot_general(left_side, right_side, (((left_dim,), (right_dim,)), ((),...]
    all_gather x1 -> x0, waiting for transfers between devices: 39.2 us -> none  [shards(): left_block = lax.all_gather(left_piece, 'col', axis=0, tiled=True)]
    all_gather x2 -> x0, blocking collectives: 38.8 us -> none  [the longest x1 31.8 us: shards(): cot_tokens = lax.all_gather(cotangent, 'col', axis=0, tiled=True)]
    psum x2 -> x0, waiting for transfers between devices: 28.4 us -> none  [the longest x1 18.5 us: shards(): lax.psum(contract(left_block, left_block, 0, 0, HIGHEST), 'row')]
    psum x1 -> x0, blocking collectives: 21.6 us -> none  [shards(): squares = lax.psum(jnp.sum(right * right, axis=0), 'col')]
    unnamed x10 -> x11, local copies, waits for them, and re-layouts: 1.03 us -> 8.26 us
  transfers between devices with their start and end apart: 5 -> 0, of which waited for: 4 -> 0; matrix products, arithmetic and copies ran while one was open for 17% -> 0% of each run, Pallas kernels for 8% -> 0%
where the time goes in v1:
time: 166 us; the launch traced here: 165 us
  Pallas kernels  156 us (94%)
  local copies, waits for them, and re-layouts  8.26 us (5%)
    pallas_call x1, Pallas kernels, left_call(): pl.pallas_call(functools.partial(left_kernel, n_row, n_col), out_shape=(j...  91.2 us
    pallas_call x1, Pallas kernels, right_call(): pl.pallas_call(functools.partial(right_kernel, n_row, n_col, ridge, din),...  52.6 us
    pallas_call x1, Pallas kernels, output_call(): pl.pallas_call(functools.partial(output_kernel, step_scale), grid=(rows /...  12.5 us
    unnamed x11, local copies, waits for them, and re-layouts  8.26 us

profile of v1, /device:TPU:0, one launch (start us, length us, event | category | flops | bytes accessed | tf_op | source)
XLA Modules:
  0.0 165.3 jit_solution(15967578389542625365)
XLA Ops:
  0.6 91.2 %left_factor.1 = (f32[8,288,256]{2,1,0:T(8,128)}, f32[256,1152]{1,0:T(8,128)}, f32[256,256]{1,0:T(8,128)}, bf16[16,1152]{1,0:T(8,128)(2,1)}, f32[2304,1152]{1,0:T(8,128)}) custom-call(bf16[16,1152]{1,0:T(8,128)(2,1)} %act_ref.1, bf16[8,2304]{1,0:T(8,128)(2,1)} %cot_ref.1, bf16[2304,1152]{1,0:T(8,128)(2,1)} %weight_hbm.1, f32[2304,1152]{1,0:T(8,128)} %momentum_hbm.1, ...), custom_call_target="tpu_custom_call" | custom-call | tf_op jit(solution)/shard_map/left_factor/pallas_call | solution.py:385
  91.9 52.6 %right_factor.1 = (f32[8,288,256]{2,1,0:T(8,128)}, f32[256,1152]{1,0:T(8,128)}, f32[8,256]{1,0:T(8,128)}) custom-call(f32[256,256]{1,0:T(8,128)} %get-tuple-element.17.gram_ref, f32[256,1152]{1,0:T(8,128)} %get-tuple-element.18.projected_ref, f32[8,288,256]{2,1,0:T(8,128)} %get-tuple-element.19.left_ref), custom_call_target="tpu_custom_call" | custom-call | tf_op jit(solution)/shard_map/right_factor/pallas_call | solution.py:560
  144.5 0.0 copy-start
  144.5 4.0 %copy-done = f32[2304,1152]{1,0:T(8,128)S(1)} copy-done((f32[2304,1152]{1,0:T(8,128)S(1)}, f32[2304,1152]{1,0:T(8,128)}, u32[]{:S(2)}) %copy-start) | copy-done | bytes 10616856
  148.5 0.0 copy-start.1
  148.5 1.7 %copy-done.1 = f32[8,288,256]{2,1,0:T(8,128)S(1)} copy-done((f32[8,288,256]{2,1,0:T(8,128)S(1)}, f32[8,288,256]{2,1,0:T(8,128)}, u32[]{:S(2)}) %copy-start.1) | copy-done | bytes 2359320
  150.2 0.0 copy-start.2
  150.2 1.3 copy-done.2
  151.5 0.0 copy-start.3
  151.5 0.7 copy-done.3
  152.2 0.0 copy-start.4
  152.2 12.5 %outputs.1 = (f32[2304,1152]{1,0:T(8,128)}, bf16[2304,1152]{1,0:T(8,128)(2,1)}, f32[1152,256]{1,0:T(8,128)}) custom-call(f32[2304,1152]{1,0:T(8,128)S(1)} %copy-done, f32[2304,256]{1,0:T(8,128)S(1)} %bitcast.1, f32[256,1152]{1,0:T(8,128)S(1)} %copy-done.2, f32[8,256]{1,0:T(8,128)S(1)} %copy-done.3), custom_call_target="tpu_custom_call" | custom-call | tf_op jit(solution)/shard_map/outputs/pallas_call | solution.py:624
  164.7 0.0 copy-done.4
  164.7 0.6 copy.10
Async XLA Ops:
  144.5 4.0 %copy-start = (f32[2304,1152]{1,0:T(8,128)S(1)}, f32[2304,1152]{1,0:T(8,128)}, u32[]{:S(2)}) copy-start(f32[2304,1152]{1,0:T(8,128)} %get-tuple-element.16.buffer_ref) | copy-start | bytes 31850500
  148.5 1.7 %copy-start.1 = (f32[8,288,256]{2,1,0:T(8,128)S(1)}, f32[8,288,256]{2,1,0:T(8,128)}, u32[]{:S(2)}) copy-start(f32[8,288,256]{2,1,0:T(8,128)} %get-tuple-element.20) | copy-start | bytes 7077892
  150.2 1.3 copy-start.2
  151.5 0.7 copy-start.3
  152.2 12.5 %copy-start.4 = (bf16[16,1152]{1,0:T(8,128)(2,1)S(1)}, bf16[16,1152]{1,0:T(8,128)(2,1)}, u32[]{:S(2)}) copy-start(bf16[16,1152]{1,0:T(8,128)(2,1)} %get-tuple-element.30) | copy-start | bytes 110596

commit v2 on v1

--- a/solution.py
+++ b/solution.py
@@ -80,6 +80,71 @@
             work[high:, :] = work[high:, :] - update[high:, :]
 
 
+def eliminate_four(groups, k, row_in_group, lanes):
+    own, inside = divmod(k, SUBLANES)
+    rows = [groups[own][inside + j : inside + j + 1, :] for j in range(4)]
+    def splat(value, j, sublanes):
+        return jnp.broadcast_to(value[:, k + j : k + j + 1], (sublanes, lanes))
+    a = [[splat(rows[i], j, 1) for j in range(i + 1)] for i in range(4)]
+    i0 = 1.0 / a[0][0]
+    i1 = a[0][0] * (1.0 / (a[0][0] * a[1][1] - a[1][0] * a[1][0]))
+    l10, l20, l30 = a[1][0] * i0, a[2][0] * i0, a[3][0] * i0
+    b21, b31 = a[2][1] - l20 * a[1][0], a[3][1] - l30 * a[1][0]
+    l21, l31 = b21 * i1, b31 * i1
+    d2 = a[2][2] - l20 * a[2][0] - l21 * b21
+    b32 = a[3][2] - l30 * a[2][0] - l31 * b21
+    s33 = a[3][3] - l30 * a[3][0] - l31 * b31
+    i2 = 1.0 / d2
+    i3 = d2 * (1.0 / (d2 * s33 - b32 * b32))
+    l32 = b32 * i2
+    u0 = rows[0]
+    u1 = rows[1] - l10 * u0
+    u2 = rows[2] - l20 * u0 - l21 * u1
+    u3 = rows[3] - l30 * u0 - l31 * u1 - l32 * u2
+    w = [u0 * i0, u1 * i1, u2 * i2, u3 * i3]
+    for g in range(own, len(groups)):
+        if g == own and inside + 4 == SUBLANES:
+            change = None
+        else:
+            c = [splat(groups[g], j, SUBLANES) for j in range(4)]
+            f1 = c[1] - c[0] * l10
+            f2 = c[2] - c[0] * l20 - f1 * l21
+            f3 = c[3] - c[0] * l30 - f1 * l31 - f2 * l32
+            change = (c[0] * w[0] + f1 * w[1]) + (f2 * w[2] + f3 * w[3])
+        if g == own:
+            value = groups[g]
+            if change is not None:
+                value = jnp.where(row_in_group > inside + 3, value - change, value)
+            for j, u in ((1, u1), (2, u2), (3, u3)):
+                value = jnp.where(row_in_group == inside + j, u, value)
+            groups[g] = value
+        else:
+            groups[g] = groups[g] - change
+
+
+def inverse_by_fours(block, ridge, gram_ref, inverse_ref, work, corner):
+    size = gram_ref.shape[0]
+    work[:, :size] = gram_ref[...] + ridge * identity(size)
+    work[:, size:] = identity(size)
+    row_in_group = lax.broadcasted_iota(jnp.int32, (SUBLANES, 2 * block), 0)
+    for low in range(0, size, block):
+        high = low + block
+        corner[:, :block] = work[low:high, low:high]
+        corner[:, block:] = identity(block)
+        groups = [corner[g : g + SUBLANES, :] for g in range(0, block, SUBLANES)]
+        for k in range(0, block, 4):
+            eliminate_four(groups, k, row_in_group, 2 * block)
+        for g, rows in enumerate(groups):
+            corner[g * SUBLANES : (g + 1) * SUBLANES, :] = rows
+        pivots = jnp.sum(corner[:, :block] * identity(block), axis=1, keepdims=True)
+        corner_inverse = corner[:, block:] * (1.0 / jnp.sqrt(pivots))
+        panel = contract(corner_inverse, work[low:high, :], 1, 0, HIGHEST)
+        inverse_ref[low:high, :] = panel[:, size:]
+        if high < size:
+            update = contract(panel[:, :size], panel, 0, 0, HIGHEST)
+            work[high:, :] = work[high:, :] - update[high:, :]
+
+
 def inverse_factor(gram_matrix, ridge):
     size = gram_matrix.shape[0]
     block = min(64, size)
@@ -146,19 +211,20 @@
     pl.semaphore_wait(barrier, len(devices))
 
 
-def left_kernel(
+def factor_kernel(
     n_row,
     n_col,
+    ridge,
     act_ref,
     cot_ref,
     weight_hbm,
     momentum_hbm,
     factor_ref,
-    left_ref,
-    projected_ref,
-    gram_ref,
     input_ref,
     buffer_hbm,
+    orthonormal_hbm,
+    right_hbm,
+    scale_ref,
     act_all,
     cot_all,
     cot_flat,
@@ -169,22 +235,49 @@
     weight,
     factor_high,
     factor_low,
+    token_high,
+    token_low,
     send_inner,
     recv_inner,
     totals,
     recv_outer,
+    left_ref,
+    gram_ref,
+    projected_ref,
     input_send,
     input_recv,
+    gram_in,
+    gram_out,
+    gram_all,
+    proj_in,
+    proj_out,
+    proj_all,
+    inverse,
+    work,
+    corner,
+    squares_all,
+    orthonormal,
+    right_ref,
     load_sem,
     store_sem,
     weight_sem,
     act_sem,
     cot_sem,
     inner_sem,
-    outer_sem,
+    chain_sem,
+    chain_in_sem,
+    gather_send_sem,
     gather_outer_sem,
     gather_inner_sem,
     input_sem,
+    gram_in_sem,
+    gram_out_sem,
+    gram_all_sem,
+    proj_in_sem,
+    proj_out_sem,
+    proj_all_sem,
+    squares_sem,
+    result_sem,
 ):
     inner, outer = two_stages(n_col)
     row, col = lax.axis_index("row"), lax.axis_index("col")
@@ -194,27 +287,31 @@
     act_rows = act_ref.shape[0]
     tokens = act_rows * n_row
 
-    def outer_id(k):
-        return lax.rem(me_out + 1 + k, outer)
+    flip = lax.div(2 * me_out, outer)
+    near = me_out + flip * (outer - 1 - 2 * me_out)
+
+    def turned_back(position):
+        return position + flip * (outer - 1 - 2 * position)
+
+    def target(k):
+        last = k // (outer - 1)
+        return turned_back(outer - 1 - k - (k + near + 1) // outer + last * (near + 1))
 
     def chunk_at(j):
-        d, k = divmod(j, outer) if isinstance(j, int) else (lax.div(j, outer), lax.rem(j, outer))
-        return outer_id(k) * inner + lax.rem(me_in + 1 + d, inner)
-
-    def load(j):
-        q = chunk_at(j)
+        return target(j % outer) * inner + (me_in + 1 + j // outer) % inner
+
+    def load(q):
         return pltpu.make_async_copy(
-            momentum_hbm.at[pl.ds(pl.multiple_of(q * piece, SUBLANES), piece), :], chunks.at[j], load_sem.at[j]
+            momentum_hbm.at[pl.ds(pl.multiple_of(q * piece, SUBLANES), piece), :], chunks.at[q], load_sem.at[q]
         )
 
-    def store(j):
-        q = chunk_at(j)
+    def store(q):
         return pltpu.make_async_copy(
-            chunks.at[j], buffer_hbm.at[pl.ds(pl.multiple_of(q * piece, SUBLANES), piece), :], store_sem.at[j]
+            chunks.at[q], buffer_hbm.at[pl.ds(pl.multiple_of(q * piece, SUBLANES), piece), :], store_sem.at[q]
         )
 
     for j in range(n_col):
-        load(j).start()
+        load(chunk_at(j)).start()
     weight_copy = pltpu.make_async_copy(weight_hbm, weight, weight_sem)
     weight_copy.start()
 
@@ -235,7 +332,33 @@
     act_all[row] = act_ref[...]
     cot_all[col] = cot_ref[...]
     factor_high[...], factor_low[...] = split(factor_ref[...])
-    for copy in act_copies + cot_copies:
+
+    def held_part(j):
+        q = chunk_at(j)
+        load(q).wait()
+        return contract_split(split(chunks[q]), (factor_high[...], factor_low[...]), 1, 0)
+
+    def turned_rows(q):
+        return cot_turned[pl.ds(pl.multiple_of(q * piece, 2 * SUBLANES), piece), :]
+
+    def token_part(j):
+        rows = turned_rows(chunk_at(j))
+        return contract(rows, token_high[...], 1, 0) + contract(rows, token_low[...], 1, 0)
+
+    for d in range(inner - 1):
+
+        def begin(k, carry, d=d):
+            send_inner[d, k] = held_part(d * outer + k)
+            return carry
+
+        lax.fori_loop(0, outer, begin, 0)
+
+    for copy in act_copies:
+        copy.wait()
+    acts = act_all[...].reshape(tokens, cols)
+    token_sums = contract(acts, factor_high[...], 1, 0) + contract(acts, factor_low[...], 1, 0)
+    token_high[...], token_low[...] = split(token_sums)
+    for copy in cot_copies:
         copy.wait()
 
     def turn(b, carry):
@@ -247,16 +370,11 @@
 
     lax.fori_loop(0, cot_ref.shape[1] // LANES, turn, 0)
 
-    def partial(j):
-        q = chunk_at(j)
-        load(j).wait()
-        turned = cot_turned[pl.ds(pl.multiple_of(q * piece, 2 * SUBLANES), piece), :]
-        value = chunks[j] + contract(turned, act_all[...].reshape(tokens, cols), 1, 0)
-        chunks[j] = value
-        high, low = split(value)
-        chunk_high[j] = high
-        chunk_low[j] = low
-        return contract_split((high, low), (factor_high[...], factor_low[...]), 1, 0)
+    def form(q):
+        value = chunks[q] + contract(turned_rows(q), act_all[...].reshape(tokens, cols), 1, 0)
+        chunks[q] = value
+        chunk_high[q], chunk_low[q] = split(value)
+        store(q).start()
 
     def inner_copy(d, k):
         peer = me_out * inner + lax.rem(me_in + 1 + d, inner)
@@ -264,27 +382,28 @@
             send_inner.at[d, k], recv_inner.at[d, k], inner_sem.at[0, d, k], inner_sem.at[1, d, k], (row, peer)
         )
 
-    def outer_copy(k):
-        peer = outer_id(k) * inner + me_in
-        return remote(totals.at[k], recv_outer.at[k], outer_sem.at[0, k], outer_sem.at[1, k], (row, peer))
+    def toward(q):
+        return 2 * ((q - me_out + outer - 1) // outer) - 1
+
+    def chain_copy(k):
+        q = target(k)
+        up = (q - me_out + outer - 1) // outer
+        ending = (outer - (me_out - q)) // (outer - 1) * (1 - up)
+        slot = q + ending * (outer - q)
+        peer = (me_out + toward(q)) * inner + me_in
+        return remote(totals.at[k], recv_outer.at[slot], chain_sem.at[k], chain_in_sem.at[slot], (row, peer))
+
+    def chain_arrival(slot):
+        return remote(totals.at[0], recv_outer.at[slot], chain_sem.at[0], chain_in_sem.at[slot], (row, col))
 
     for d in range(inner - 1):
 
         def push(k, carry, d=d):
-            send_inner[d, k] = partial(d * outer + k)
+            send_inner[d, k] = send_inner[d, k] + token_part(d * outer + k)
             inner_copy(d, k).start()
             return carry
 
         lax.fori_loop(0, outer, push, 0)
-
-    def keep(k, carry):
-        totals[k] = partial((inner - 1) * outer + k)
-        return carry
-
-    lax.fori_loop(0, outer, keep, 0)
-
-    for j in range(n_col):
-        store(j).start()
 
     weight_copy.wait()
     input_part = contract(cot_flat[...], weight[...], 1, 0)
@@ -296,187 +415,152 @@
     for copy in input_copies:
         copy.start()
 
-    for k in range(outer):
-        total = totals[k]
+    def own_part(k):
+        j = (inner - 1) * outer + k
+        value = held_part(j) + token_part(j)
+        for d in range(inner):
+            form(chunk_at(d * outer + k))
+        return value
+
+    def chain(k, carry):
+        total = own_part(k)
         for d in range(inner - 1):
-            inner_copy(d, k).wait()
+            inner_copy(d, k).wait_recv()
             total = total + recv_inner[d, k]
         totals[k] = total
-        if k < outer - 1:
-            outer_copy(k).start()
-    mine = totals[outer - 1]
-    for k in range(outer - 1):
-        outer_copy(k).wait()
-        mine = mine + recv_outer[k]
-    left_ref[col] = mine / jnp.sqrt(jnp.float32(din))
-
-    def gather_outer(k):
-        peer = outer_id(k) * inner + me_in
+        q = target(k)
+
+        @pl.when(jnp.logical_and(me_out - toward(q) >= 0, me_out - toward(q) < outer))
+        def _():
+            chain_arrival(q).wait_recv()
+            totals[k] = totals[k] + recv_outer[q]
+
+        chain_copy(k).start()
+        return carry
+
+    lax.fori_loop(0, outer - 1, chain, 0)
+    mine = own_part(outer - 1)
+    for d in range(inner - 1):
+        inner_copy(d, outer - 1).wait_recv()
+        mine = mine + recv_inner[d, outer - 1]
+    totals[outer - 1] = mine
+
+    @pl.when(me_out > 0)
+    def _():
+        chain_arrival(me_out).wait_recv()
+        totals[outer - 1] = totals[outer - 1] + recv_outer[me_out]
+
+    @pl.when(me_out < outer - 1)
+    def _():
+        chain_arrival(outer).wait_recv()
+        totals[outer - 1] = totals[outer - 1] + recv_outer[outer]
+
+    left_ref[col] = totals[outer - 1] / jnp.sqrt(jnp.float32(din))
+
+    def gather_outer(q, up):
+        piece_ref = left_ref.at[q * inner + me_in]
+        peer = (me_out + 2 * up - 1) * inner + me_in
+        return remote(piece_ref, piece_ref, gather_send_sem.at[up, q], gather_outer_sem.at[q], (row, peer))
+
+    def gather_inner(d, q):
+        piece_ref = left_ref.at[q * inner + me_in]
+        peer = me_out * inner + (me_in + 1 + d) % inner
         return remote(
-            left_ref.at[col], left_ref.at[col], gather_outer_sem.at[0, k], gather_outer_sem.at[1, k], (row, peer)
+            piece_ref, piece_ref, gather_inner_sem.at[0, d, q], gather_inner_sem.at[1, d, q], (row, peer)
         )
 
-    def source_outer(k):
-        return lax.rem(me_out + outer - k, outer)
-
-    def gather_inner(d, k):
-        q = source_outer(k) * inner + me_in
-        peer = me_out * inner + lax.rem(me_in + 1 + d, inner)
-        return remote(
-            left_ref.at[q], left_ref.at[q], gather_inner_sem.at[0, d, k], gather_inner_sem.at[1, d, k], (row, peer)
-        )
-
-    for k in range(outer - 1):
-        gather_outer(k).start()
+    def onward(q, start):
+        up = 1 - (q - me_out + outer - 1) // outer
+
+        @pl.when(jnp.logical_and(me_out + 2 * up - 1 >= 0, me_out + 2 * up - 1 < outer))
+        def _():
+            copy = gather_outer(q, up)
+            copy.start() if start else copy.wait_send()
+
+    def own_outward(start):
+        for up in range(2):
+
+            @pl.when(jnp.logical_and(me_out + 2 * up - 1 >= 0, me_out + 2 * up - 1 < outer))
+            def _():
+                copy = gather_outer(me_out, up)
+                copy.start() if start else copy.wait_send()
+
+    own_outward(True)
     for d in range(inner - 1):
-        gather_inner(d, 0).start()
-
-    def place(q):
-        d = lax.rem(lax.rem(q, inner) - me_in - 1 + 2 * inner, inner)
-        k = lax.rem(lax.div(q, inner) - me_out - 1 + 2 * outer, outer)
-        return d * outer + k
-
-    def absorb(q, first):
+        gather_inner(d, me_out).start()
+
+    def arrival(n):
+        paired = (2 * near - n - 1 + 2 * outer) // (2 * outer)
+        step = (n // 2 + 1) * (2 * (n % 2) - 1)
+        return turned_back(paired * (near + step) + (1 - paired) * (n + 1))
+
+    def absorb(q):
         value = left_ref[q]
         pair = split(value)
-        j = place(q)
-        gram = contract(value, value, 0, 0, HIGHEST)
-        projected = contract_split(pair, (chunk_high[j], chunk_low[j]), 0, 0)
-        if first:
-            gram_ref[...] = gram
-            projected_ref[...] = projected
-        else:
-            gram_ref[...] = gram_ref[...] + gram
-            projected_ref[...] = projected_ref[...] + projected
-
-    absorb(col, True)
-    for k in range(1, outer):
-        gather_outer(k - 1).wait()
+        gram_ref[...] = gram_ref[...] + contract(value, value, 0, 0, HIGHEST)
+        projected_ref[...] = projected_ref[...] + contract_split(pair, (chunk_high[q], chunk_low[q]), 0, 0)
+
+    def absorb_inner(d, q):
+        gather_inner(d, q).wait_recv()
+        absorb(q * inner + (me_in - 1 - d + inner) % inner)
+
+    gram_ref[...] = jnp.zeros_like(gram_ref)
+    projected_ref[...] = jnp.zeros_like(projected_ref)
+    absorb(col)
+
+    def gather(n, before):
+        q = arrival(n)
+        gather_outer(q, 0).wait_recv()
+        onward(q, True)
         for d in range(inner - 1):
-            gather_inner(d, k).start()
-        absorb(source_outer(k) * inner + me_in, False)
+            gather_inner(d, q).start()
+        absorb(q * inner + me_in)
         for d in range(inner - 1):
-            gather_inner(d, k - 1).wait()
-            absorb(source_outer(k - 1) * inner + lax.rem(me_in - 1 - d + inner, inner), False)
+            absorb_inner(d, before)
+        return q
+
+    final = lax.fori_loop(0, outer - 1, gather, me_out)
     for d in range(inner - 1):
-        gather_inner(d, outer - 1).wait()
-        absorb(source_outer(outer - 1) * inner + lax.rem(me_in - 1 - d + inner, inner), False)
-
-    total = input_send[row]
-    for d, copy in enumerate(input_copies):
-        copy.wait()
-        total = total + input_recv[d]
-    input_ref[...] = total.astype(jnp.bfloat16)
-    for j in range(n_col):
-        store(j).wait()
-
-
-def left_call(n_row, n_col, activations, cotangent, weight, momentum, right_factor):
-    inner, outer = two_stages(n_col)
-    rows, cols = momentum.shape
-    rank = right_factor.shape[1]
-    piece = rows // n_col
-    act_rows, cot_rows = activations.shape[0], cotangent.shape[0]
-    tokens = act_rows * n_row
-    f32, bf16 = jnp.float32, jnp.bfloat16
-    vmem = pl.BlockSpec(memory_space=pltpu.VMEM)
-    hbm = pl.BlockSpec(memory_space=pl.ANY)
-    dma = pltpu.SemaphoreType.DMA
-    return pl.pallas_call(
-        functools.partial(left_kernel, n_row, n_col),
-        out_shape=(
-            jax.ShapeDtypeStruct((n_col, piece, rank), f32),
-            jax.ShapeDtypeStruct((rank, cols), f32),
-            jax.ShapeDtypeStruct((rank, rank), f32),
-            jax.ShapeDtypeStruct((act_rows, cols), bf16),
-            jax.ShapeDtypeStruct((rows, cols), f32),
-        ),
-        in_specs=[vmem, vmem, hbm, hbm, vmem],
-        out_specs=(vmem, vmem, vmem, vmem, hbm),
-        scratch_shapes=[
-            pltpu.VMEM((n_row, act_rows, cols), bf16),
-            pltpu.VMEM((n_col, cot_rows, rows), bf16),
-            pltpu.VMEM((tokens, rows), bf16),
-            pltpu.VMEM((rows, tokens), bf16),
-            pltpu.VMEM((n_col, piece, cols), f32),
-            pltpu.VMEM((n_col, piece, cols), bf16),
-            pltpu.VMEM((n_col, piece, cols), bf16),
-            pltpu.VMEM((rows, cols), bf16),
-            pltpu.VMEM((cols, rank), bf16),
-            pltpu.VMEM((cols, rank), bf16),
-            pltpu.VMEM((inner - 1, outer, piece, rank), f32),
-            pltpu.VMEM((inner - 1, outer, piece, rank), f32),
-            pltpu.VMEM((outer, piece, rank), f32),
-            pltpu.VMEM((outer - 1, piece, rank), f32),
-            pltpu.VMEM((n_row, act_rows, cols), f32),
-            pltpu.VMEM((n_row - 1, act_rows, cols), f32),
-            dma((n_col,)),
-            dma((n_col,)),
-            dma,
-            dma((2, n_row - 1)),
-            dma((2, n_col - 1)),
-            dma((2, inner - 1, outer)),
-            dma((2, outer - 1)),
-            dma((2, outer - 1)),
-            dma((2, inner - 1, outer)),
-            dma((2, n_row - 1)),
-        ],
-        compiler_params=pltpu.CompilerParams(
-            collective_id=1, has_side_effects=True, vmem_limit_bytes=60 * 1024 * 1024
-        ),
-        name="left_factor",
-    )(activations, cotangent, weight, momentum, right_factor)
-
-
-def right_kernel(
-    n_row,
-    n_col,
-    ridge,
-    din,
-    gram_ref,
-    projected_ref,
-    left_ref,
-    orthonormal_ref,
-    right_ref,
-    scale_ref,
-    gram_in,
-    gram_out,
-    gram_all,
-    proj_in,
-    proj_out,
-    proj_all,
-    inverse,
-    work,
-    corner,
-    squares_all,
-    gram_in_sem,
-    gram_out_sem,
-    gram_all_sem,
-    proj_in_sem,
-    proj_out_sem,
-    proj_all_sem,
-    squares_sem,
-):
-    inner, outer = two_stages(n_row)
-    row, col = lax.axis_index("row"), lax.axis_index("col")
-    me_in, me_out = lax.rem(row, inner), lax.div(row, inner)
+        absorb_inner(d, final)
+
+    def finish():
+        total = input_send[row]
+        for d, copy in enumerate(input_copies):
+            copy.wait()
+            total = total + input_recv[d]
+        input_ref[...] = total.astype(jnp.bfloat16)
+        for q in range(n_col):
+            store(q).wait()
+
+        def drain(k, carry):
+            for d in range(inner - 1):
+                inner_copy(d, k).wait_send()
+                gather_inner(d, k).wait_send()
+            return carry
+
+        lax.fori_loop(0, outer, drain, 0)
+
+        def drain_chain(k, carry):
+            chain_copy(k).wait_send()
+            onward(arrival(k), False)
+            return carry
+
+        lax.fori_loop(0, outer - 1, drain_chain, 0)
+        own_outward(False)
+
+
     rank = gram_ref.shape[0]
-    part = rank // inner
-    inner_peers = [(lax.rem(me_in + 1 + d, inner)) for d in range(inner - 1)]
-    outer_peers = [(lax.rem(me_out + 1 + d, outer)) for d in range(outer - 1)]
-    col_peers = [lax.rem(col + d, n_col) for d in range(1, n_col)]
-    greet(
-        [(me_out * inner + peer, col) for peer in inner_peers]
-        + [(peer * inner + me_in, col) for peer in outer_peers]
-        + [(row, peer) for peer in col_peers]
-    )
-
+    row_inner, row_outer = two_stages(n_row)
+    row_me_in, row_me_out = lax.rem(row, row_inner), lax.div(row, row_inner)
+    part = rank // row_inner
+    inner_peers = [(lax.rem(row_me_in + 1 + d, row_inner)) for d in range(row_inner - 1)]
+    outer_peers = [(lax.rem(row_me_out + 1 + d, row_outer)) for d in range(row_outer - 1)]
     def at(index):
         return pl.ds(pl.multiple_of(index * part, SUBLANES), part)
 
     def reduce_in(source, buffer, sem):
         copies = [
-            remote(source.at[at(peer), :], buffer.at[d], sem.at[0, d], sem.at[1, d], (me_out * inner + peer, col))
+            remote(source.at[at(peer), :], buffer.at[d], sem.at[0, d], sem.at[1, d], (row_me_out * row_inner + peer, col))
             for d, peer in enumerate(inner_peers)
         ]
         for copy in copies:
@@ -484,14 +568,14 @@
         return copies
 
     def exchange_out(source, copies_in, buffer_in, buffer_out, sem):
-        total = source[at(me_in), :]
+        total = source[at(row_me_in), :]
         for d, copy in enumerate(copies_in):
             copy.wait()
             total = total + buffer_in[d]
-        buffer_out[me_out] = total
+        buffer_out[row_me_out] = total
         copies = [
             remote(
-                buffer_out.at[me_out], buffer_out.at[me_out], sem.at[0, d], sem.at[1, d], (peer * inner + me_in, col)
+                buffer_out.at[row_me_out], buffer_out.at[row_me_out], sem.at[0, d], sem.at[1, d], (peer * row_inner + row_me_in, col)
             )
             for d, peer in enumerate(outer_peers)
         ]
@@ -503,12 +587,12 @@
         for copy in copies_out:
             copy.wait()
         total = buffer_out[0]
-        for o in range(1, outer):
+        for o in range(1, row_outer):
             total = total + buffer_out[o]
-        whole[at(me_in), :] = total
+        whole[at(row_me_in), :] = total
         copies = [
             remote(
-                whole.at[at(me_in), :], whole.at[at(me_in), :], sem.at[0, d], sem.at[1, d], (me_out * inner + peer, col)
+                whole.at[at(row_me_in), :], whole.at[at(row_me_in), :], sem.at[0, d], sem.at[1, d], (row_me_out * row_inner + peer, col)
             )
             for d, peer in enumerate(inner_peers)
         ]
@@ -520,14 +604,13 @@
     proj_copies = reduce_in(projected_ref, proj_in, proj_in_sem)
     gram_copies = exchange_out(gram_ref, gram_copies, gram_in, gram_out, gram_out_sem)
     proj_copies = exchange_out(projected_ref, proj_copies, proj_in, proj_out, proj_out_sem)
+    finish()
     gram_copies = gather_in(gram_copies, gram_out, gram_all, gram_all_sem)
     for copy in gram_copies:
         copy.wait()
-    inverse_factor_body(corner.shape[0], ridge, gram_all, inverse, work, corner)
+    inverse_by_fours(corner.shape[0], ridge, gram_all, inverse, work, corner)
     proj_copies = gather_in(proj_copies, proj_out, proj_all, proj_all_sem)
     factor = split(inverse[...])
-    for q in range(n_col):
-        orthonormal_ref[q] = contract_split(split(left_ref[q]), factor, 1, 1)
     for copy in proj_copies:
         copy.wait()
     right = contract_split(factor, split(proj_all[...]), 1, 0)
@@ -541,55 +624,114 @@
     ]
     for copy in copies:
         copy.start()
+    right_copy = pltpu.make_async_copy(right_ref, right_hbm, result_sem.at[n_col])
+    right_copy.start()
+
+    def result(q):
+        return pltpu.make_async_copy(orthonormal.at[q], orthonormal_hbm.at[q], result_sem.at[q])
+
+    def orthonormalise(q, carry):
+        orthonormal[q] = contract_split(split(left_ref[q]), factor, 1, 1)
+        result(q).start()
+        return carry
+
+    lax.fori_loop(0, n_col, orthonormalise, 0)
     for copy in copies:
         copy.wait()
     total = squares_all[0]
     for q in range(1, n_col):
         total = total + squares_all[q]
     scale_ref[...] = lax.rsqrt(total / din + 1e-06)
-
-
-def right_call(n_row, n_col, ridge, din, gram_part, projected_part, left):
-    inner, outer = two_stages(n_row)
-    rank, cols = projected_part.shape
-    part = rank // inner
+    right_copy.wait()
+    for q in range(n_col):
+        result(q).wait()
+
+
+def factor_call(n_row, n_col, ridge, activations, cotangent, weight, momentum, right_factor):
+    inner, outer = two_stages(n_col)
+    row_inner, row_outer = two_stages(n_row)
+    rows, cols = momentum.shape
+    rank = right_factor.shape[1]
+    piece = rows // n_col
+    part = rank // row_inner
     block = min(64, rank)
-    f32 = jnp.float32
+    act_rows, cot_rows = activations.shape[0], cotangent.shape[0]
+    tokens = act_rows * n_row
+    f32, bf16 = jnp.float32, jnp.bfloat16
     vmem = pl.BlockSpec(memory_space=pltpu.VMEM)
+    hbm = pl.BlockSpec(memory_space=pl.ANY)
     dma = pltpu.SemaphoreType.DMA
     return pl.pallas_call(
-        functools.partial(right_kernel, n_row, n_col, ridge, din),
+        functools.partial(factor_kernel, n_row, n_col, ridge),
         out_shape=(
-            jax.ShapeDtypeStruct(left.shape, f32),
+            jax.ShapeDtypeStruct((act_rows, cols), bf16),
+            jax.ShapeDtypeStruct((rows, cols), f32),
+            jax.ShapeDtypeStruct((n_col, piece, rank), f32),
             jax.ShapeDtypeStruct((rank, cols), f32),
             jax.ShapeDtypeStruct((SUBLANES, rank), f32),
         ),
-        in_specs=[vmem] * 3,
-        out_specs=(vmem,) * 3,
+        in_specs=[vmem, vmem, hbm, hbm, vmem],
+        out_specs=(vmem, hbm, hbm, hbm, vmem),
         scratch_shapes=[
-            pltpu.VMEM((inner - 1, part, rank), f32),
-            pltpu.VMEM((outer, part, rank), f32),
+            pltpu.VMEM((n_row, act_rows, cols), bf16),
+            pltpu.VMEM((n_col, cot_rows, rows), bf16),
+            pltpu.VMEM((tokens, rows), bf16),
+            pltpu.VMEM((rows, tokens), bf16),
+            pltpu.VMEM((n_col, piece, cols), f32),
+            pltpu.VMEM((n_col, piece, cols), bf16),
+            pltpu.VMEM((n_col, piece, cols), bf16),
+            pltpu.VMEM((rows, cols), bf16),
+            pltpu.VMEM((cols, rank), bf16),
+            pltpu.VMEM((cols, rank), bf16),
+            pltpu.VMEM((tokens, rank), bf16),
+            pltpu.VMEM((tokens, rank), bf16),
+            pltpu.VMEM((inner - 1, outer, piece, rank), f32),
+            pltpu.VMEM((inner - 1, outer, piece, rank), f32),
+            pltpu.VMEM((outer, piece, rank), f32),
+            pltpu.VMEM((outer + 1, piece, rank), f32),
+            pltpu.VMEM((n_col, piece, rank), f32),
             pltpu.VMEM((rank, rank), f32),
-            pltpu.VMEM((inner - 1, part, cols), f32),
-            pltpu.VMEM((outer, part, cols), f32),
+            pltpu.VMEM((rank, cols), f32),
+            pltpu.VMEM((n_row, act_rows, cols), f32),
+            pltpu.VMEM((n_row - 1, act_rows, cols), f32),
+            pltpu.VMEM((row_inner - 1, part, rank), f32),
+            pltpu.VMEM((row_outer, part, rank), f32),
+            pltpu.VMEM((rank, rank), f32),
+            pltpu.VMEM((row_inner - 1, part, cols), f32),
+            pltpu.VMEM((row_outer, part, cols), f32),
             pltpu.VMEM((rank, cols), f32),
             pltpu.VMEM((rank, rank), f32),
             pltpu.VMEM((rank, 2 * rank), f32),
             pltpu.VMEM((block, 2 * block), f32),
             pltpu.VMEM((n_col, SUBLANES, rank), f32),
-            dma((2, inner - 1)),
-            dma((2, outer - 1)),
-            dma((2, inner - 1)),
-            dma((2, inner - 1)),
-            dma((2, outer - 1)),
-            dma((2, inner - 1)),
+            pltpu.VMEM((n_col, piece, rank), f32),
+            pltpu.VMEM((rank, cols), f32),
+            dma((n_col,)),
+            dma((n_col,)),
+            dma,
+            dma((2, n_row - 1)),
             dma((2, n_col - 1)),
+            dma((2, inner - 1, outer)),
+            dma((outer,)),
+            dma((outer + 1,)),
+            dma((2, outer)),
+            dma((outer,)),
+            dma((2, inner - 1, outer)),
+            dma((2, n_row - 1)),
+            dma((2, row_inner - 1)),
+            dma((2, row_outer - 1)),
+            dma((2, row_inner - 1)),
+            dma((2, row_inner - 1)),
+            dma((2, row_outer - 1)),
+            dma((2, row_inner - 1)),
+            dma((2, n_col - 1)),
+            dma((n_col + 1,)),
         ],
         compiler_params=pltpu.CompilerParams(
-            collective_id=2, has_side_effects=True, vmem_limit_bytes=60 * 1024 * 1024
+            collective_id=1, has_side_effects=True, vmem_limit_bytes=60 * 1024 * 1024
         ),
-        name="right_factor",
-    )(gram_part, projected_part, left)
+        name="factors",
+    )(activations, cotangent, weight, momentum, right_factor)
 
 
 def output_kernel(
@@ -642,7 +784,7 @@
         ),
         scratch_shapes=[pltpu.VMEM((rank, cols), jnp.bfloat16), pltpu.VMEM((rank, cols), jnp.bfloat16)],
         compiler_params=pltpu.CompilerParams(
-            dimension_semantics=("arbitrary",), vmem_limit_bytes=40 * 1024 * 1024
+            dimension_semantics=("arbitrary",), vmem_limit_bytes=60 * 1024 * 1024
         ),
         name="outputs",
     )(buffer, orthonormal, right, scale)
@@ -651,11 +793,10 @@
 def kernel_shards(n_row, n_col, activations, cotangent, weight, momentum, right_factor):
     rows, cols = momentum.shape
     rank = right_factor.shape[1]
-    dout, din = rows * n_row, cols * n_col
-    left, projected, gram, input_grad, buffer = left_call(
-        n_row, n_col, activations, cotangent, weight, momentum, right_factor
+    dout = rows * n_row
+    input_grad, buffer, orthonormal, right, scale = factor_call(
+        n_row, n_col, ridge_weight * dout, activations, cotangent, weight, momentum, right_factor
     )
-    orthonormal, right, scale = right_call(n_row, n_col, ridge_weight * dout, din, gram, projected, left)
     step_scale = (dout / rank) ** 0.5
     momentum_next, weight_step, right_next = output_call(
         step_scale, buffer, orthonormal.reshape(rows, rank), right, scale

time: 166 us -> 126 us (0.76)
  Pallas kernels: 156 us -> 124 us
  local copies, waits for them, and re-layouts: 8.26 us -> 0.62 us
    pallas_call x2 -> x1, Pallas kernels: 144 us -> 108 us  [factor_call(): pl.pallas_call(functools.partial(factor_kernel, n_row, n_col, ridge), out...]
    unnamed x11 -> x3, local copies, waits for them, and re-layouts: 8.26 us -> 0.62 us
    pallas_call x1, Pallas kernels: 12.5 us -> 16 us  [output_call(): pl.pallas_call(functools.partial(output_kernel, step_scale), grid=(rows /...]
where the time goes in v2:
time: 126 us; the launch traced here: 125 us
  Pallas kernels  124 us (98%)
    pallas_call x1, Pallas kernels, factor_call(): pl.pallas_call(functools.partial(factor_kernel, n_row, n_col, ridge), out...  108 us
    pallas_call x1, Pallas kernels, output_call(): pl.pallas_call(functools.partial(output_kernel, step_scale), grid=(rows /...  16 us

profile of v2, /device:TPU:0, one launch (start us, length us, event | category | flops | bytes accessed | tf_op | source)
XLA Modules:
  0.0 125.2 jit_solution(14328261758347348490)
XLA Ops:
  0.6 107.9 %factors.1 = (bf16[16,1152]{1,0:T(8,128)(2,1)}, f32[2304,1152]{1,0:T(8,128)}, f32[8,288,256]{2,1,0:T(8,128)}, f32[256,1152]{1,0:T(8,128)}, f32[8,256]{1,0:T(8,128)}) custom-call(bf16[16,1152]{1,0:T(8,128)(2,1)} %act_ref.1, bf16[8,2304]{1,0:T(8,128)(2,1)} %cot_ref.1, bf16[2304,1152]{1,0:T(8,128)(2,1)} %weight_hbm.1, f32[2304,1152]{1,0:T(8,128)} %momentum_hbm.1, ...), custom_call_target="tpu_custom_call" | custom-call | tf_op jit(solution)/shard_map/factors/pallas_call | solution.py:664
  108.5 0.0 copy-start
  108.5 16.0 %outputs.1 = (f32[2304,1152]{1,0:T(8,128)}, bf16[2304,1152]{1,0:T(8,128)(2,1)}, f32[1152,256]{1,0:T(8,128)}) custom-call(f32[2304,1152]{1,0:T(8,128)} %get-tuple-element.13.buffer_ref, f32[2304,256]{1,0:T(8,128)} %bitcast.1, f32[256,1152]{1,0:T(8,128)} %get-tuple-element.15.right_ref, f32[8,256]{1,0:T(8,128)} %get-tuple-element.16.scale_ref), custom_call_target="tpu_custom_call" | custom-call | tf_op jit(solution)/shard_map/outputs/pallas_call | solution.py:766
  124.6 0.0 copy-done
  124.6 0.6 copy.10
Async XLA Ops:
  108.5 16.0 %copy-start = (bf16[16,1152]{1,0:T(8,128)(2,1)S(1)}, bf16[16,1152]{1,0:T(8,128)(2,1)}, u32[]{:S(2)}) copy-start(bf16[16,1152]{1,0:T(8,128)(2,1)} %get-tuple-element.24) | copy-start | bytes 110596

commit v3 on v2

v3 whole, which is shorter than its diff:
```python
import functools

import jax
import jax.numpy as jnp
from jax import lax
from jax.experimental import pallas as pl
from jax.experimental.pallas import tpu as pltpu
from jax.sharding import PartitionSpec as P

momentum_decay = 0.6
ridge_weight = 0.001

HIGHEST = lax.Precision.HIGHEST
HIGH = lax.Precision.HIGH
SUBLANES = 8
LANES = 128
MESH = pl.DeviceIdType.MESH


def contract(left_side, right_side, left_dim, right_dim, precision=None):
    return lax.dot_general(
        left_side,
        right_side,
        (((left_dim,), (right_dim,)), ((), ())),
        precision=precision,
        preferred_element_type=jnp.float32,
    )


def identity(size):
    shape = (size, size)
    same = lax.broadcasted_iota(jnp.int32, shape, 0) == lax.broadcasted_iota(jnp.int32, shape, 1)
    return jnp.where(same, 1.0, 0.0).astype(jnp.float32)


def two_stages(size):
    inner = max(k for k in range(1, size + 1) if size % k == 0 and k * k <= size)
    return inner, size // inner


def split(value):
    high = value.astype(jnp.bfloat16)
    return high, (value - high.astype(jnp.float32)).astype(jnp.bfloat16)


def contract_split(left_pair, right_pair, left_dim, right_dim):
    total = contract(left_pair[0], right_pair[0], left_dim, right_dim)
    total = total + contract(left_pair[1], right_pair[0], left_dim, right_dim)
    return total + contract(left_pair[0], right_pair[1], left_dim, right_dim)


def inverse_factor_body(block, ridge, gram_ref, inverse_ref, work, corner):
    size = gram_ref.shape[0]
    work[:, :size] = gram_ref[...] + ridge * identity(size)
    work[:, size:] = identity(size)
    row_in_group = lax.broadcasted_iota(jnp.int32, (SUBLANES, 2 * block), 0)
    for low in range(0, size, block):
        high = low + block
        corner[:, :block] = work[low:high, low:high]
        corner[:, block:] = identity(block)
        groups = [corner[g : g + SUBLANES, :] for g in range(0, block, SUBLANES)]
        for k in range(block):
            own, inside = divmod(k, SUBLANES)
            pivot_row = groups[own][inside : inside + 1, :]
            scaled = pivot_row / pivot_row[:, k : k + 1]
            for g in range(own, len(groups)):
                factor = groups[g][:, k : k + 1]
                change = factor * scaled
                if g == own:
                    change = jnp.where(row_in_group > inside, change, 0.0)
                groups[g] = groups[g] - change
        for g, rows in enumerate(groups):
            corner[g * SUBLANES : (g + 1) * SUBLANES, :] = rows
        pivots = jnp.sum(corner[:, :block] * identity(block), axis=1, keepdims=True)
        corner_inverse = corner[:, block:] * (1.0 / jnp.sqrt(pivots))
        panel = contract(corner_inverse, work[low:high, :], 1, 0, HIGHEST)
        inverse_ref[low:high, :] = panel[:, size:]
        if high < size:
            update = contract(panel[:, :size], panel, 0, 0, HIGHEST)
            work[high:, :] = work[high:, :] - update[high:, :]


def eliminate_four(groups, k, row_in_group, lanes):
    own, inside = divmod(k, SUBLANES)
    rows = [groups[own][inside + j : inside + j + 1, :] for j in range(4)]
    def splat(value, j, sublanes):
        return jnp.broadcast_to(value[:, k + j : k + j + 1], (sublanes, lanes))
    a = [[splat(rows[i], j, 1) for j in range(i + 1)] for i in range(4)]
    i0 = 1.0 / a[0][0]
    i1 = a[0][0] * (1.0 / (a[0][0] * a[1][1] - a[1][0] * a[1][0]))
    l10, l20, l30 = a[1][0] * i0, a[2][0] * i0, a[3][0] * i0
    b21, b31 = a[2][1] - l20 * a[1][0], a[3][1] - l30 * a[1][0]
    l21, l31 = b21 * i1, b31 * i1
    d2 = a[2][2] - l20 * a[2][0] - l21 * b21
    b32 = a[3][2] - l30 * a[2][0] - l31 * b21
    s33 = a[3][3] - l30 * a[3][0] - l31 * b31
    i2 = 1.0 / d2
    i3 = d2 * (1.0 / (d2 * s33 - b32 * b32))
    l32 = b32 * i2
    u0 = rows[0]
    u1 = rows[1] - l10 * u0
    u2 = rows[2] - l20 * u0 - l21 * u1
    u3 = rows[3] - l30 * u0 - l31 * u1 - l32 * u2
    w = [u0 * i0, u1 * i1, u2 * i2, u3 * i3]
    for g in range(own, len(groups)):
        if g == own and inside + 4 == SUBLANES:
            change = None
        else:
            c = [splat(groups[g], j, SUBLANES) for j in range(4)]
            f1 = c[1] - c[0] * l10
            f2 = c[2] - c[0] * l20 - f1 * l21
            f3 = c[3] - c[0] * l30 - f1 * l31 - f2 * l32
            change = (c[0] * w[0] + f1 * w[1]) + (f2 * w[2] + f3 * w[3])
        if g == own:
            value = groups[g]
            if change is not None:
                value = jnp.where(row_in_group > inside + 3, value - change, value)
            for j, u in ((1, u1), (2, u2), (3, u3)):
                value = jnp.where(row_in_group == inside + j, u, value)
            groups[g] = value
        else:
            groups[g] = groups[g] - change


def invert_block(low, block, work, corner, inverse_ref):
    size = work.shape[0]
    high = low + block
    row_in_group = lax.broadcasted_iota(jnp.int32, (SUBLANES, 2 * block), 0)
    corner[:, :block] = work[low:high, low:high]
    corner[:, block:] = identity(block)
    groups = [corner[g : g + SUBLANES, :] for g in range(0, block, SUBLANES)]
    for k in range(0, block, 4):
        eliminate_four(groups, k, row_in_group, 2 * block)
    for g, rows in enumerate(groups):
        corner[g * SUBLANES : (g + 1) * SUBLANES, :] = rows
    pivots = jnp.sum(corner[:, :block] * identity(block), axis=1, keepdims=True)
    corner_inverse = corner[:, block:] * (1.0 / jnp.sqrt(pivots))
    panel = contract(corner_inverse, work[low:high, :], 1, 0, HIGHEST)
    inverse_ref[low:high, :] = panel[:, size:]
    if high < size:
        update = contract(panel[:, :size], panel, 0, 0, HIGHEST)
        work[high:, :] = work[high:, :] - update[high:, :]


def inverse_factor(gram_matrix, ridge):
    size = gram_matrix.shape[0]
    block = min(64, size)
    return pl.pallas_call(
        functools.partial(inverse_factor_body, block, ridge),
        out_shape=jax.ShapeDtypeStruct((size, size), jnp.float32),
        in_specs=[pl.BlockSpec(memory_space=pltpu.VMEM)],
        out_specs=pl.BlockSpec(memory_space=pltpu.VMEM),
        scratch_shapes=[
            pltpu.VMEM((size, 2 * size), jnp.float32),
            pltpu.VMEM((block, 2 * block), jnp.float32),
        ],
        cost_estimate=pl.CostEstimate(flops=20_000_000_000, bytes_accessed=8 * size * size, transcendentals=0),
        name="inverse_factor",
    )(gram_matrix)


def plain_shards(rows_of, cols_of, activations, cotangent, weight, momentum, right_factor):
    dout = momentum.shape[0] * rows_of
    din = momentum.shape[1] * cols_of
    rank = right_factor.shape[1]
    cot_tokens = lax.all_gather(cotangent, "col", axis=0, tiled=True)
    act_tokens = lax.all_gather(activations, "row", axis=0, tiled=True)
    held_part = contract(momentum, right_factor, 1, 0, HIGH)
    act_part = contract(act_tokens.astype(jnp.float32), right_factor, 1, 0, HIGH)
    grad_part = contract(cot_tokens.astype(jnp.float32), act_part, 0, 0, HIGH)
    left_part = (held_part + grad_part) / jnp.sqrt(jnp.float32(din))
    left_piece = lax.psum_scatter(left_part, "col", scatter_dimension=0, tiled=True)
    input_part = jnp.dot(cot_tokens, weight, preferred_element_type=jnp.float32)
    buffer = momentum + contract(cot_tokens, act_tokens, 0, 0, None)
    left_block = lax.all_gather(left_piece, "col", axis=0, tiled=True)
    gram_matrix = lax.psum(contract(left_block, left_block, 0, 0, HIGHEST), "row")
    projected_part = contract(buffer, left_block, 0, 0, HIGH)
    gram_matrix, projected_part = lax.optimization_barrier((gram_matrix, projected_part))
    projected = lax.psum(projected_part, "row")
    projected, input_part = lax.optimization_barrier((projected, input_part))
    input_sums = lax.psum_scatter(input_part, "row", scatter_dimension=0, tiled=True)
    inverse = inverse_factor(gram_matrix, ridge_weight * dout)
    orthonormal = contract(left_block, inverse, 1, 1, HIGHEST)
    right = contract(projected, inverse, 1, 1, HIGHEST)
    squares = lax.psum(jnp.sum(right * right, axis=0), "col")
    momentum_next = buffer - (1.0 - momentum_decay) * contract(orthonormal, right, 1, 1, HIGH)
    right_next = right * lax.rsqrt(squares / din + 1e-06)
    step_scale = jnp.sqrt(jnp.float32(dout) / rank)
    weight_step = (step_scale * contract(orthonormal, right_next, 1, 1, HIGH)).astype(jnp.bfloat16)
    return (input_sums.astype(jnp.bfloat16), momentum_next, right_next, weight_step)


def remote(source, target, send_sem, recv_sem, device):
    return pltpu.make_async_remote_copy(
        src_ref=source,
        dst_ref=target,
        send_sem=send_sem,
        recv_sem=recv_sem,
        device_id=device,
        device_id_type=MESH,
    )


def greet(devices):
    barrier = pltpu.get_barrier_semaphore()
    for device in devices:
        pl.semaphore_signal(barrier, inc=1, device_id=device, device_id_type=MESH)
    pl.semaphore_wait(barrier, len(devices))


def factor_kernel(
    n_row,
    n_col,
    ridge,
    act_ref,
    cot_ref,
    weight_hbm,
    momentum_hbm,
    factor_ref,
    input_ref,
    buffer_hbm,
    orthonormal_hbm,
    right_high_hbm,
    right_low_hbm,
    right_turned_hbm,
    scale_ref,
    act_all,
    cot_all,
    cot_flat,
    cot_turned,
    chunks,
    chunk_high,
    chunk_low,
    weight,
    factor_high,
    factor_low,
    token_send,
    token_recv,
    token_high,
    token_low,
    send_inner,
    recv_inner,
    totals,
    recv_outer,
    left_ref,
    gram_ref,
    projected_ref,
    input_send,
    input_recv,
    gram_in,
    gram_out,
    gram_all,
    proj_in,
    proj_out,
    proj_all,
    inverse,
    diagonal,
    work,
    corner,
    squares_all,
    orthonormal,
    right_high,
    right_low,
    right_turned,
    load_sem,
    store_sem,
    weight_sem,
    act_sem,
    cot_sem,
    token_sem,
    inner_sem,
    chain_sem,
    chain_in_sem,
    gather_send_sem,
    gather_outer_sem,
    gather_inner_sem,
    input_sem,
    gram_in_sem,
    gram_out_sem,
    gram_all_sem,
    proj_in_sem,
    proj_out_sem,
    proj_all_sem,
    squares_sem,
    result_sem,
):
    inner, outer = two_stages(n_col)
    row_inner, row_outer = two_stages(n_row)
    row, col = lax.axis_index("row"), lax.axis_index("col")
    me_in, me_out = lax.rem(col, inner), lax.div(col, inner)
    row_in, row_out = lax.rem(row, row_inner), lax.div(row, row_inner)
    piece, cols = chunks.shape[1], chunks.shape[2]
    halves, width = left_ref.shape[0], left_ref.shape[3]
    rank = halves * width
    din = cols * n_col
    act_rows = act_ref.shape[0]
    tokens = act_rows * n_row
    flip = lax.div(2 * me_out, outer)
    near = me_out + flip * (outer - 1 - 2 * me_out)

    def lanes_of(h):
        return slice(h * width, (h + 1) * width)

    def turned_back(position):
        return position + flip * (outer - 1 - 2 * position)

    def target(k):
        last = k // (outer - 1)
        return turned_back(outer - 1 - k - (k + near + 1) // outer + last * (near + 1))

    def chunk_at(j):
        return target(j % outer) * inner + (me_in + 1 + j // outer) % inner

    def load(q):
        return pltpu.make_async_copy(
            momentum_hbm.at[pl.ds(pl.multiple_of(q * piece, SUBLANES), piece), :], chunks.at[q], load_sem.at[q]
        )

    def store(q):
        return pltpu.make_async_copy(
            chunks.at[q], buffer_hbm.at[pl.ds(pl.multiple_of(q * piece, SUBLANES), piece), :], store_sem.at[q]
        )

    for j in range(n_col):
        load(chunk_at(j)).start()
    weight_copy = pltpu.make_async_copy(weight_hbm, weight, weight_sem)
    weight_copy.start()
    factor_high[...], factor_low[...] = split(factor_ref[...])

    row_peers = [lax.rem(row + d, n_row) for d in range(1, n_row)]
    col_peers = [lax.rem(col + d, n_col) for d in range(1, n_col)]
    greet([(peer, col) for peer in row_peers] + [(row, peer) for peer in col_peers])

    cot_copies = [
        remote(cot_ref, cot_all.at[col], cot_sem.at[0, d], cot_sem.at[1, d], (row, peer))
        for d, peer in enumerate(col_peers)
    ]
    act_copies = [
        remote(act_ref, act_all.at[row], act_sem.at[0, d], act_sem.at[1, d], (peer, col))
        for d, peer in enumerate(row_peers)
    ]
    for copy in cot_copies + act_copies:
        copy.start()
    act_all[row] = act_ref[...]
    cot_all[col] = cot_ref[...]

    def held_part(j):
        q = chunk_at(j)
        load(q).wait()
        return contract_split(split(chunks[q]), (factor_high[...], factor_low[...]), 1, 0)

    def turned_rows(q):
        return cot_turned[pl.ds(pl.multiple_of(q * piece, 2 * SUBLANES), piece), :]

    def token_part(j):
        rows = turned_rows(chunk_at(j))
        return contract(rows, token_high[...], 1, 0) + contract(rows, token_low[...], 1, 0)

    def inner_copy(h, d, k):
        peer = me_out * inner + (me_in + 1 + d) % inner
        return remote(
            send_inner.at[h, d, k],
            recv_inner.at[h, d, k],
            inner_sem.at[0, h, d, k],
            inner_sem.at[1, h, d, k],
            (row, peer),
        )

    def push(d, k):
        value = held_part(d * outer + k)
        for h in range(halves):
            send_inner[h, d, k] = value[:, lanes_of(h)]
        inner_copy(0, d, k).start()

    push(0, 0)
    for copy in act_copies:
        copy.wait()
    acts = act_all[...].reshape(tokens, cols)
    token_send[...] = contract(acts, factor_high[...], 1, 0) + contract(acts, factor_low[...], 1, 0)
    token_copies = [
        remote(
            token_send,
            token_recv.at[d],
            token_sem.at[0, d],
            token_sem.at[1, d],
            (row, me_out * inner + (me_in + 1 + d) % inner),
        )
        for d in range(inner - 1)
    ]
    for copy in token_copies:
        copy.start()
    for d in range(inner - 1):

        def push_next(k, carry, d=d):
            push(d, k)
            return carry

        lax.fori_loop(1 if d == 0 else 0, outer, push_next, 0)
    for h in range(1, halves):
        for d in range(inner - 1):

            def push_half(k, carry, h=h, d=d):
                inner_copy(h, d, k).start()
                return carry

            lax.fori_loop(0, outer, push_half, 0)
    for copy in cot_copies:
        copy.wait()

    def turn(b, carry):
        lanes = pl.ds(pl.multiple_of(b * LANES, LANES), LANES)
        slab = cot_all[:, :, lanes].astype(jnp.float32).reshape(tokens, LANES)
        cot_flat[:, lanes] = slab.astype(jnp.bfloat16)
        cot_turned[lanes, :] = slab.T.astype(jnp.bfloat16)
        return carry

    lax.fori_loop(0, cot_ref.shape[1] // LANES, turn, 0)

    token_sums = token_send[...]
    for d, copy in enumerate(token_copies):
        copy.wait()
        token_sums = token_sums + token_recv[d]
    token_high[...], token_low[...] = split(token_sums)

    def form(q):
        value = chunks[q] + contract(turned_rows(q), act_all[...].reshape(tokens, cols), 1, 0)
        chunks[q] = value
        chunk_high[q], chunk_low[q] = split(value)
        store(q).start()

    def own_part(k):
        j = (inner - 1) * outer + k
        value = held_part(j) + token_part(j)
        for h in range(halves):
            totals[h, k] = value[:, lanes_of(h)]

    def toward(q):
        return 2 * ((q - me_out + outer - 1) // outer) - 1

    def chain_copy(h, k):
        q = target(k)
        up = (q - me_out + outer - 1) // outer
        ending = (outer - (me_out - q)) // (outer - 1) * (1 - up)
        slot = q + ending * (outer - q)
        peer = (me_out + toward(q)) * inner + me_in
        return remote(
            totals.at[h, k], recv_outer.at[h, slot], chain_sem.at[h, k], chain_in_sem.at[h, slot], (row, peer)
        )

    def chain_arrival(h, slot):
        return remote(
            totals.at[h, 0], recv_outer.at[h, slot], chain_sem.at[h, 0], chain_in_sem.at[h, slot], (row, col)
        )

    def add_inner(h, k):
        for d in range(inner - 1):
            inner_copy(h, d, k).wait_recv()
            totals[h, k] = totals[h, k] + recv_inner[h, d, k]

    def chain(h, k):
        add_inner(h, k)
        q = target(k)

        @pl.when(jnp.logical_and(me_out - toward(q) >= 0, me_out - toward(q) < outer))
        def _():
            chain_arrival(h, q).wait_recv()
            totals[h, k] = totals[h, k] + recv_outer[h, q]

        chain_copy(h, k).start()

    def gather_outer(h, q, up):
        piece_ref = left_ref.at[h, q * inner + me_in]
        peer = (me_out + 2 * up - 1) * inner + me_in
        return remote(piece_ref, piece_ref, gather_send_sem.at[h, up, q], gather_outer_sem.at[h, q], (row, peer))

    def gather_inner(h, d, q):
        piece_ref = left_ref.at[h, q * inner + me_in]
        peer = me_out * inner + (me_in + 1 + d) % inner
        return remote(
            piece_ref, piece_ref, gather_inner_sem.at[0, h, d, q], gather_inner_sem.at[1, h, d, q], (row, peer)
        )

    def onward(h, q, start):
        up = 1 - (q - me_out + outer - 1) // outer

        @pl.when(jnp.logical_and(me_out + 2 * up - 1 >= 0, me_out + 2 * up - 1 < outer))
        def _():
            copy = gather_outer(h, q, up)
            copy.start() if start else copy.wait_send()

    def own_outward(h, start):
        for up in range(2):

            @pl.when(jnp.logical_and(me_out + 2 * up - 1 >= 0, me_out + 2 * up - 1 < outer))
            def _():
                copy = gather_outer(h, me_out, up)
                copy.start() if start else copy.wait_send()

    def settle(h):
        add_inner(h, outer - 1)

        @pl.when(me_out > 0)
        def _():
            chain_arrival(h, me_out).wait_recv()
            totals[h, outer - 1] = totals[h, outer - 1] + recv_outer[h, me_out]

        @pl.when(me_out < outer - 1)
        def _():
            chain_arrival(h, outer).wait_recv()
            totals[h, outer - 1] = totals[h, outer - 1] + recv_outer[h, outer]

        left_ref[h, col] = totals[h, outer - 1] / jnp.sqrt(jnp.float32(din))
        own_outward(h, True)
        for d in range(inner - 1):
            gather_inner(h, d, me_out).start()

    def arrival(n):
        paired = (2 * near - n - 1 + 2 * outer) // (2 * outer)
        step = (n // 2 + 1) * (2 * (n % 2) - 1)
        return turned_back(paired * (near + step) + (1 - paired) * (n + 1))

    def forward(h, n):
        q = arrival(n)
        gather_outer(h, q, 0).wait_recv()
        onward(h, q, True)
        for d in range(inner - 1):
            gather_inner(h, d, q).start()

    def absorb(h, q):
        value = left_ref[h, q]
        for g in range(h + 1):
            gram_ref[h, :, lanes_of(g)] = gram_ref[h, :, lanes_of(g)] + contract(value, left_ref[g, q], 0, 0, HIGHEST)
        projected_ref[h] = projected_ref[h] + contract_split(split(value), (chunk_high[q], chunk_low[q]), 0, 0)

    def absorb_outer(h, n):
        absorb(h, arrival(n) * inner + me_in)

    def absorb_inner(h, q):
        for d in range(inner - 1):
            gather_inner(h, d, q).wait_recv()
            absorb(h, q * inner + (me_in - 1 - d + inner) % inner)

    part = width // row_inner
    inner_peers = [lax.rem(row_in + 1 + d, row_inner) for d in range(row_inner - 1)]
    outer_peers = [lax.rem(row_out + 1 + d, row_outer) for d in range(row_outer - 1)]

    def rows_at(index):
        return pl.ds(pl.multiple_of(index * part, SUBLANES), part)

    class RowSum:
        def __init__(self, source, buffer_in, buffer_out, whole, sems, h, span):
            self.source, self.whole, self.h = source, whole, h
            self.buffer_in, self.buffer_out, self.lanes = buffer_in, buffer_out, pl.ds(0, span)
            self.sems = sems

        def view(self, ref, index, rows=None):
            if rows is None:
                return ref.at[self.h, index, :, self.lanes]
            return ref.at[self.h, rows, self.lanes]

        def begin(self):
            sem = self.sems[0]
            self.first = [
                remote(
                    self.view(self.source, None, rows_at(peer)),
                    self.view(self.buffer_in, d),
                    sem.at[0, self.h, d],
                    sem.at[1, self.h, d],
                    (row_out * row_inner + peer, col),
                )
                for d, peer in enumerate(inner_peers)
            ]
            for copy in self.first:
                copy.start()

        def cross(self):
            sem = self.sems[1]
            total = self.source[self.h, rows_at(row_in), self.lanes]
            for d, copy in enumerate(self.first):
                copy.wait()
                total = total + self.buffer_in[self.h, d, :, self.lanes]
            self.buffer_out[self.h, row_out, :, self.lanes] = total
            mine = self.view(self.buffer_out, row_out)
            self.second = [
                remote(mine, mine, sem.at[0, self.h, d], sem.at[1, self.h, d], (peer * row_inner + row_in, col))
                for d, peer in enumerate(outer_peers)
            ]
            for copy in self.second:
                copy.start()

        def spread(self):
            sem = self.sems[2]
            for copy in self.second:
                copy.wait()
            total = self.buffer_out[self.h, 0, :, self.lanes]
            for o in range(1, row_outer):
                total = total + self.buffer_out[self.h, o, :, self.lanes]
            self.whole[self.h, rows_at(row_in), self.lanes] = total
            mine = self.view(self.whole, None, rows_at(row_in))
            self.third = [
                remote(mine, mine, sem.at[0, self.h, d], sem.at[1, self.h, d], (row_out * row_inner + peer, col))
                for d, peer in enumerate(inner_peers)
            ]
            for copy in self.third:
                copy.start()

        def end(self):
            for copy in self.third:
                copy.wait()

    gram_sums = [
        RowSum(gram_ref, gram_in, gram_out, gram_all, (gram_in_sem, gram_out_sem, gram_all_sem), h, (h + 1) * width)
        for h in range(halves)
    ]
    proj_sums = [
        RowSum(projected_ref, proj_in, proj_out, proj_all, (proj_in_sem, proj_out_sem, proj_all_sem), h, cols)
        for h in range(halves)
    ]
    block = corner.shape[0]

    def prepare_half(h):
        known = h * width
        shift = ridge * identity(width)
        gram = gram_all[h, :, known : known + width]
        if h == 0:
            inverse[...] = jnp.zeros_like(inverse)
            rest = None
        else:
            before = inverse[:known, :known]
            solved = contract(before, gram_all[h, :, :known], 1, 1, HIGHEST)
            gram = gram - contract(solved, solved, 0, 0, HIGHEST)
            rest = contract(solved, before, 0, 0, HIGHEST)
        work[:, :width] = gram + shift
        work[:, width:] = identity(width)
        return rest

    def finish_half(h, rest):
        known = h * width
        inverse[known : known + width, known : known + width] = diagonal[...]
        if h > 0:
            inverse[known : known + width, :known] = -contract(diagonal[...], rest, 1, 0, HIGHEST)

    def right_half(h):
        known = (h + 1) * width
        projected = proj_all[: h + 1].reshape(known, cols)
        factor = split(inverse[h * width : known, :known])
        right = contract_split(factor, split(projected), 1, 0)
        right_high[lanes_of(h), :], right_low[lanes_of(h), :] = split(right)
        squares = jnp.sum(right * right, axis=1, keepdims=True)
        squares_all[col, :, lanes_of(h)] = jnp.broadcast_to(squares, (width, LANES)).T[:SUBLANES, :]
        return right

    gram_ref[...] = jnp.zeros_like(gram_ref)
    projected_ref[...] = jnp.zeros_like(projected_ref)

    def open_chain(k, carry):
        own_part(k)
        chain(0, k)
        return carry

    lax.fori_loop(0, outer - 1, open_chain, 0)
    own_part(outer - 1)

    def form_some(q, carry):
        form(q)
        return carry

    lax.fori_loop(0, n_col // 2, form_some, 0)
    settle(0)
    weight_copy.wait()
    input_part = contract(cot_flat[...], weight[...], 1, 0)
    input_send[...] = input_part.reshape(n_row, act_rows, cols)
    input_copies = [
        remote(input_send.at[peer], input_recv.at[d], input_sem.at[0, d], input_sem.at[1, d], (peer, col))
        for d, peer in enumerate(row_peers)
    ]
    for copy in input_copies:
        copy.start()
    chain(1, 0)
    lax.fori_loop(n_col // 2, n_col, form_some, 0)

    def next_chain(k, carry):
        chain(1, k)
        forward(0, k - 1)
        return carry

    lax.fori_loop(1, outer - 1, next_chain, 0)
    absorb(0, col)
    settle(1)
    forward(0, outer - 2)

    def absorb_first(n, carry):
        absorb_outer(0, n)
        return carry

    lax.fori_loop(0, outer - 1, absorb_first, 0)
    absorb_inner(0, me_out)
    absorb(1, col)

    def absorb_second(n, carry):
        forward(1, n)
        absorb_inner(0, arrival(n))
        absorb_outer(1, n)
        return carry

    lax.fori_loop(0, outer - 2, absorb_second, 0)
    absorb_inner(0, arrival(outer - 2))
    gram_sums[0].begin()
    proj_sums[0].begin()
    absorb_inner(1, me_out)
    gram_sums[0].cross()
    proj_sums[0].cross()
    forward(1, outer - 2)
    absorb_outer(1, outer - 2)
    gram_sums[0].spread()

    def absorb_third(n, carry):
        absorb_inner(1, arrival(n))
        return carry

    lax.fori_loop(0, outer - 1, absorb_third, 0)
    gram_sums[1].begin()
    proj_sums[1].begin()
    gram_sums[0].end()
    gram_sums[1].cross()
    proj_sums[0].spread()
    proj_sums[1].cross()
    rest = prepare_half(0)
    for low in range(0, width, block):
        invert_block(low, block, work, corner, diagonal)
        if low == 0:
            gram_sums[1].spread()
    finish_half(0, rest)
    proj_sums[0].end()
    right_turned_parts = [right_half(0)]
    gram_sums[1].end()
    rest = prepare_half(1)
    for low in range(0, width, block):
        invert_block(low, block, work, corner, diagonal)
        if low == 0:
            proj_sums[1].spread()
    finish_half(1, rest)
    proj_sums[1].end()
    right_turned_parts.append(right_half(1))

    copies = [
        remote(squares_all.at[col], squares_all.at[col], squares_sem.at[0, d], squares_sem.at[1, d], (row, peer))
        for d, peer in enumerate(col_peers)
    ]
    for copy in copies:
        copy.start()

    for h in range(halves):
        right_turned[:, lanes_of(h)] = right_turned_parts[h].T

    def result(q):
        return pltpu.make_async_copy(orthonormal.at[q], orthonormal_hbm.at[q], result_sem.at[q])

    right_copies = [
        pltpu.make_async_copy(right_high, right_high_hbm, result_sem.at[n_col]),
        pltpu.make_async_copy(right_low, right_low_hbm, result_sem.at[n_col + 1]),
        pltpu.make_async_copy(right_turned, right_turned_hbm, result_sem.at[n_col + 2]),
    ]
    for copy in right_copies:
        copy.start()

    def orthonormalise(q, carry):
        total = contract_split(split(left_ref[0, q]), split(inverse[:, :width]), 1, 1)
        for h in range(1, halves):
            total = total + contract_split(split(left_ref[h, q]), split(inverse[:, lanes_of(h)]), 1, 1)
        orthonormal[q] = total
        result(q).start()
        return carry

    lax.fori_loop(0, n_col, orthonormalise, 0)
    total = input_send[row]
    for d, copy in enumerate(input_copies):
        copy.wait()
        total = total + input_recv[d]
    input_ref[...] = total.astype(jnp.bfloat16)
    for q in range(n_col):
        store(q).wait()

    for h in range(halves):

        def drain(k, carry, h=h):
            for d in range(inner - 1):
                inner_copy(h, d, k).wait_send()
                gather_inner(h, d, k).wait_send()
            return carry

        lax.fori_loop(0, outer, drain, 0)

        def drain_chain(k, carry, h=h):
            chain_copy(h, k).wait_send()
            onward(h, arrival(k), False)
            return carry

        lax.fori_loop(0, outer - 1, drain_chain, 0)
        own_outward(h, False)

    for copy in copies:
        copy.wait()
    total = squares_all[0]
    for q in range(1, n_col):
        total = total + squares_all[q]
    scale_ref[...] = lax.rsqrt(total / din + 1e-06)
    for copy in right_copies:
        copy.wait()
    for q in range(n_col):
        result(q).wait()


def factor_call(n_row, n_col, ridge, activations, cotangent, weight, momentum, right_factor):
    inner, outer = two_stages(n_col)
    row_inner, row_outer = two_stages(n_row)
    rows, cols = momentum.shape
    rank = right_factor.shape[1]
    halves, width = 2, rank // 2
    piece = rows // n_col
    part = width // row_inner
    block = min(64, width)
    act_rows, cot_rows = activations.shape[0], cotangent.shape[0]
    tokens = act_rows * n_row
    f32, bf16 = jnp.float32, jnp.bfloat16
    vmem = pl.BlockSpec(memory_space=pltpu.VMEM)
    hbm = pl.BlockSpec(memory_space=pl.ANY)
    dma = pltpu.SemaphoreType.DMA
    return pl.pallas_call(
        functools.partial(factor_kernel, n_row, n_col, ridge),
        out_shape=(
            jax.ShapeDtypeStruct((act_rows, cols), bf16),
            jax.ShapeDtypeStruct((rows, cols), f32),
            jax.ShapeDtypeStruct((n_col, piece, rank), f32),
            jax.ShapeDtypeStruct((rank, cols), bf16),
            jax.ShapeDtypeStruct((rank, cols), bf16),
            jax.ShapeDtypeStruct((cols, rank), f32),
            jax.ShapeDtypeStruct((SUBLANES, rank), f32),
        ),
        in_specs=[vmem, vmem, hbm, hbm, vmem],
        out_specs=(vmem, hbm, hbm, hbm, hbm, hbm, vmem),
        scratch_shapes=[
            pltpu.VMEM((n_row, act_rows, cols), bf16),
            pltpu.VMEM((n_col, cot_rows, rows), bf16),
            pltpu.VMEM((tokens, rows), bf16),
            pltpu.VMEM((rows, tokens), bf16),
            pltpu.VMEM((n_col, piece, cols), f32),
            pltpu.VMEM((n_col, piece, cols), bf16),
            pltpu.VMEM((n_col, piece, cols), bf16),
            pltpu.VMEM((rows, cols), bf16),
            pltpu.VMEM((cols, rank), bf16),
            pltpu.VMEM((cols, rank), bf16),
            pltpu.VMEM((tokens, rank), f32),
            pltpu.VMEM((inner - 1, tokens, rank), f32),
            pltpu.VMEM((tokens, rank), bf16),
            pltpu.VMEM((tokens, rank), bf16),
            pltpu.VMEM((halves, inner - 1, outer, piece, width), f32),
            pltpu.VMEM((halves, inner - 1, outer, piece, width), f32),
            pltpu.VMEM((halves, outer, piece, width), f32),
            pltpu.VMEM((halves, outer + 1, piece, width), f32),
            pltpu.VMEM((halves, n_col, piece, width), f32),
            pltpu.VMEM((halves, width, rank), f32),
            pltpu.VMEM((halves, width, cols), f32),
            pltpu.VMEM((n_row, act_rows, cols), f32),
            pltpu.VMEM((n_row - 1, act_rows, cols), f32),
            pltpu.VMEM((halves, row_inner - 1, part, rank), f32),
            pltpu.VMEM((halves, row_outer, part, rank), f32),
            pltpu.VMEM((halves, width, rank), f32),
            pltpu.VMEM((halves, row_inner - 1, part, cols), f32),
            pltpu.VMEM((halves, row_outer, part, cols), f32),
            pltpu.VMEM((halves, width, cols), f32),
            pltpu.VMEM((rank, rank), f32),
            pltpu.VMEM((width, width), f32),
            pltpu.VMEM((width, 2 * width), f32),
            pltpu.VMEM((block, 2 * block), f32),
            pltpu.VMEM((n_col, SUBLANES, rank), f32),
            pltpu.VMEM((n_col, piece, rank), f32),
            pltpu.VMEM((rank, cols), bf16),
            pltpu.VMEM((rank, cols), bf16),
            pltpu.VMEM((cols, rank), f32),
            dma((n_col,)),
            dma((n_col,)),
            dma,
            dma((2, n_row - 1)),
            dma((2, n_col - 1)),
            dma((2, inner - 1)),
            dma((2, halves, inner - 1, outer)),
            dma((halves, outer)),
            dma((halves, outer + 1)),
            dma((halves, 2, outer)),
            dma((halves, outer)),
            dma((2, halves, inner - 1, outer)),
            dma((2, n_row - 1)),
            dma((2, halves, row_inner - 1)),
            dma((2, halves, row_outer - 1)),
            dma((2, halves, row_inner - 1)),
            dma((2, halves, row_inner - 1)),
            dma((2, halves, row_outer - 1)),
            dma((2, halves, row_inner - 1)),
            dma((2, n_col - 1)),
            dma((n_col + 3,)),
        ],
        compiler_params=pltpu.CompilerParams(
            collective_id=1, has_side_effects=True, vmem_limit_bytes=60 * 1024 * 1024
        ),
        name="factors",
    )(activations, cotangent, weight, momentum, right_factor)


def output_kernel(
    step_scale,
    buffer_ref,
    orthonormal_ref,
    right_high_ref,
    right_low_ref,
    right_turned_ref,
    scale_ref,
    momentum_ref,
    step_ref,
    next_ref,
):
    right = (right_high_ref[...], right_low_ref[...])
    orthonormal = orthonormal_ref[...]
    momentum_ref[...] = buffer_ref[...] - (1.0 - momentum_decay) * contract_split(split(orthonormal), right, 1, 0)
    scaled = orthonormal * scale_ref[:1, :]
    step_ref[...] = (step_scale * contract_split(split(scaled), right, 1, 0)).astype(jnp.bfloat16)
    next_ref[...] = right_turned_ref[...] * scale_ref[:1, :]


def output_tile(rows, cols):
    fits = [t for t in range(16, 289, 16) if rows % t == 0 and cols % (rows // t * SUBLANES) == 0]
    return max(fits, default=0)


def output_call(step_scale, buffer, orthonormal, right_high, right_low, right_turned, scale):
    rows, cols = buffer.shape
    rank = right_high.shape[0]
    tile = output_tile(rows, cols)
    steps = rows // tile
    f32 = jnp.float32
    whole = pl.BlockSpec((rank, cols), lambda i: (0, 0))
    return pl.pallas_call(
        functools.partial(output_kernel, step_scale),
        grid=(steps,),
        out_shape=(
            jax.ShapeDtypeStruct((rows, cols), f32),
            jax.ShapeDtypeStruct((rows, cols), jnp.bfloat16),
            jax.ShapeDtypeStruct((cols, rank), f32),
        ),
        in_specs=[
            pl.BlockSpec((tile, cols), lambda i: (i, 0)),
            pl.BlockSpec((tile, rank), lambda i: (i, 0)),
            whole,
            whole,
            pl.BlockSpec((cols // steps, rank), lambda i: (i, 0)),
            pl.BlockSpec(scale.shape, lambda i: (0, 0)),
        ],
        out_specs=(
            pl.BlockSpec((tile, cols), lambda i: (i, 0)),
            pl.BlockSpec((tile, cols), lambda i: (i, 0)),
            pl.BlockSpec((cols // steps, rank), lambda i: (i, 0)),
        ),
        compiler_params=pltpu.CompilerParams(
            dimension_semantics=("arbitrary",), vmem_limit_bytes=60 * 1024 * 1024
        ),
        name="outputs",
    )(buffer, orthonormal, right_high, right_low, right_turned, scale)


def kernel_shards(n_row, n_col, activations, cotangent, weight, momentum, right_factor):
    rows, cols = momentum.shape
    rank = right_factor.shape[1]
    dout = rows * n_row
    input_grad, buffer, orthonormal, right_high, right_low, right_turned, scale = factor_call(
        n_row, n_col, ridge_weight * dout, activations, cotangent, weight, momentum, right_factor
    )
    step_scale = (dout / rank) ** 0.5
    momentum_next, weight_step, right_next = output_call(
        step_scale, buffer, orthonormal.reshape(rows, rank), right_high, right_low, right_turned, scale
    )
    return input_grad, momentum_next, right_next, weight_step


def shards(n_row, n_col, activations, cotangent, weight, momentum, right_factor):
    rows, cols = momentum.shape
    rank = right_factor.shape[1]
    aligned = (
        rows % (n_col * 2 * SUBLANES) == 0
        and rows % LANES == 0
        and cols % LANES == 0
        and rank % (2 * LANES) == 0
        and output_tile(rows, cols) > 0
        and activations.shape[0] % (2 * SUBLANES) == 0
        and cotangent.shape[0] % SUBLANES == 0
        and two_stages(n_row)[0] > 1
        and two_stages(n_col)[0] > 1
        and n_col % 2 == 0
        and rank % (2 * two_stages(n_row)[0] * SUBLANES) == 0
    )
    chosen = kernel_shards if aligned else plain_shards
    return chosen(n_row, n_col, activations, cotangent, weight, momentum, right_factor)


def solution(mesh):
    placed = (P("row", "col"), P("col", "row"), P("row", "col"), P("row", "col"), P("col", None))
    return jax.shard_map(
        functools.partial(shards, mesh.shape["row"], mesh.shape["col"]),
        mesh=mesh,
        in_specs=placed,
        out_specs=(P("row", "col"), P("row", "col"), P("col", None), P("row", "col")),
        check_vma=False,
    )
```

time: 126 us -> 113 us (0.90)
  Pallas kernels: 124 us -> 111 us
    pallas_call x1, Pallas kernels: 108 us -> 95.2 us  [factor_call(): pl.pallas_call(functools.partial(factor_kernel, n_row, n_col, ridge), out...]
where the time goes in v3:
time: 113 us; the launch traced here: 112 us
  Pallas kernels  111 us (98%)
    pallas_call x1, Pallas kernels, factor_call(): pl.pallas_call(functools.partial(factor_kernel, n_row, n_col, ridge), out...  95.2 us
    pallas_call x1, Pallas kernels, output_call(): pl.pallas_call(functools.partial(output_kernel, step_scale), grid=(steps,...  15.9 us

profile of v3, /device:TPU:0, one launch (start us, length us, event | category | flops | bytes accessed | tf_op | source)
XLA Modules:
  0.0 112.4 jit_solution(18258157707237167017)
XLA Ops:
  0.6 95.2 %factors.1 = (bf16[16,1152]{1,0:T(8,128)(2,1)}, f32[2304,1152]{1,0:T(8,128)}, f32[8,288,256]{2,1,0:T(8,128)}, bf16[256,1152]{1,0:T(8,128)(2,1)}, bf16[256,1152]{...) custom-call(bf16[16,1152]{1,0:T(8,128)(2,1)} %act_ref.1, bf16[8,2304]{1,0:T(8,128)(2,1)} %cot_ref.1, ...), custom_call_target="tpu_custom_call" | custom-call | tf_op jit(solution)/shard_map/factors/pallas_call | solution.py:829
  95.9 0.0 copy-start
  95.9 15.9 %outputs.1 = (f32[2304,1152]{1,0:T(8,128)}, bf16[2304,1152]{1,0:T(8,128)(2,1)}, f32[1152,256]{1,0:T(8,128)}) custom-call(f32[2304,1152]{1,0:T(8,128)} %get-tuple-element.15.buffer_ref, f32[2304,256]{1,0:T(8,128)} %bitcast.1, bf16[256,1152]{1,0:T(8,128)(2,1)} %get-tuple-element.17.right_high_ref, bf16[256,1152]{1,0:T(8,128)(2,1)} %get-tuple-element.18.right_low_ref, ...), custom_call_target="tpu_custom_call" | custom-call | tf_op jit(solution)/shard_map/outputs/pallas_call | solution.py:942
  111.8 0.0 copy-done
  111.8 0.6 copy.10
Async XLA Ops:
  95.9 15.9 %copy-start = (bf16[16,1152]{1,0:T(8,128)(2,1)S(1)}, bf16[16,1152]{1,0:T(8,128)(2,1)}, u32[]{:S(2)}) copy-start(bf16[16,1152]{1,0:T(8,128)(2,1)} %get-tuple-element.28) | copy-start | bytes 110596

commit v4 on v3

--- a/solution.py
+++ b/solution.py
@@ -516,7 +516,7 @@
 
     def arrival(n):
         paired = (2 * near - n - 1 + 2 * outer) // (2 * outer)
-        step = (n // 2 + 1) * (2 * (n % 2) - 1)
+        step = (n // 2 + 1) * (1 - 2 * (n % 2))
         return turned_back(paired * (near + step) + (1 - paired) * (n + 1))
 
     def forward(h, n):
@@ -666,6 +666,11 @@
         return carry
 
     lax.fori_loop(0, n_col // 2, form_some, 0)
+
+    @pl.when(near == 0)
+    def _():
+        chain(1, 0)
+
     settle(0)
     weight_copy.wait()
     input_part = contract(cot_flat[...], weight[...], 1, 0)
@@ -676,15 +681,31 @@
     ]
     for copy in input_copies:
         copy.start()
-    chain(1, 0)
     lax.fori_loop(n_col // 2, n_col, form_some, 0)
 
     def next_chain(k, carry):
+        chain(1, k)
+        return carry
+
+    def next_forward(n, carry):
+        forward(0, n)
+        return carry
+
+    def next_both(k, carry):
         chain(1, k)
         forward(0, k - 1)
         return carry
 
-    lax.fori_loop(1, outer - 1, next_chain, 0)
+    @pl.when(near == 0)
+    def _():
+        lax.fori_loop(1, outer - 1, next_chain, 0)
+        lax.fori_loop(0, outer - 2, next_forward, 0)
+
+    @pl.when(near > 0)
+    def _():
+        chain(1, 0)
+        lax.fori_loop(1, outer - 1, next_both, 0)
+
     absorb(0, col)
     settle(1)
     forward(0, outer - 2)
@@ -723,13 +744,13 @@
     proj_sums[1].begin()
     gram_sums[0].end()
     gram_sums[1].cross()
-    proj_sums[0].spread()
     proj_sums[1].cross()
     rest = prepare_half(0)
     for low in range(0, width, block):
         invert_block(low, block, work, corner, diagonal)
         if low == 0:
             gram_sums[1].spread()
+    proj_sums[0].spread()
     finish_half(0, rest)
     proj_sums[0].end()
     right_turned_parts = [right_half(0)]
@@ -915,24 +936,31 @@
     right_low_ref,
     right_turned_ref,
     scale_ref,
+    sums_ref,
     momentum_ref,
     step_ref,
     next_ref,
+    input_ref,
 ):
-    right = (right_high_ref[...], right_low_ref[...])
+    input_ref[...] = sums_ref[...]
+    right = jnp.concatenate([right_high_ref[...], right_high_ref[...], right_low_ref[...]], axis=0)
+
+    def product(value):
+        high, low = split(value)
+        return contract(jnp.concatenate([high, low, high], axis=1), right, 1, 0)
+
     orthonormal = orthonormal_ref[...]
-    momentum_ref[...] = buffer_ref[...] - (1.0 - momentum_decay) * contract_split(split(orthonormal), right, 1, 0)
-    scaled = orthonormal * scale_ref[:1, :]
-    step_ref[...] = (step_scale * contract_split(split(scaled), right, 1, 0)).astype(jnp.bfloat16)
+    momentum_ref[...] = buffer_ref[...] - (1.0 - momentum_decay) * product(orthonormal)
+    step_ref[...] = (step_scale * product(orthonormal * scale_ref[:1, :])).astype(jnp.bfloat16)
     next_ref[...] = right_turned_ref[...] * scale_ref[:1, :]
 
 
 def output_tile(rows, cols):
-    fits = [t for t in range(16, 289, 16) if rows % t == 0 and cols % (rows // t * SUBLANES) == 0]
+    fits = [t for t in range(16, min(rows // 4, 576) + 1, 16) if rows % t == 0 and cols % (rows // t * SUBLANES) == 0]
     return max(fits, default=0)
 
 
-def output_call(step_scale, buffer, orthonormal, right_high, right_low, right_turned, scale):
+def output_call(step_scale, buffer, orthonormal, right_high, right_low, right_turned, scale, sums):
     rows, cols = buffer.shape
     rank = right_high.shape[0]
     tile = output_tile(rows, cols)
@@ -946,6 +974,7 @@
             jax.ShapeDtypeStruct((rows, cols), f32),
             jax.ShapeDtypeStruct((rows, cols), jnp.bfloat16),
             jax.ShapeDtypeStruct((cols, rank), f32),
+            jax.ShapeDtypeStruct(sums.shape, sums.dtype),
         ),
         in_specs=[
             pl.BlockSpec((tile, cols), lambda i: (i, 0)),
@@ -954,29 +983,31 @@
             whole,
             pl.BlockSpec((cols // steps, rank), lambda i: (i, 0)),
             pl.BlockSpec(scale.shape, lambda i: (0, 0)),
+            pl.BlockSpec(sums.shape, lambda i: (0, 0)),
         ],
         out_specs=(
             pl.BlockSpec((tile, cols), lambda i: (i, 0)),
             pl.BlockSpec((tile, cols), lambda i: (i, 0)),
             pl.BlockSpec((cols // steps, rank), lambda i: (i, 0)),
+            pl.BlockSpec(sums.shape, lambda i: (0, 0)),
         ),
         compiler_params=pltpu.CompilerParams(
             dimension_semantics=("arbitrary",), vmem_limit_bytes=60 * 1024 * 1024
         ),
         name="outputs",
-    )(buffer, orthonormal, right_high, right_low, right_turned, scale)
+    )(buffer, orthonormal, right_high, right_low, right_turned, scale, sums)
 
 
 def kernel_shards(n_row, n_col, activations, cotangent, weight, momentum, right_factor):
     rows, cols = momentum.shape
     rank = right_factor.shape[1]
     dout = rows * n_row
-    input_grad, buffer, orthonormal, right_high, right_low, right_turned, scale = factor_call(
+    input_sums, buffer, orthonormal, right_high, right_low, right_turned, scale = factor_call(
         n_row, n_col, ridge_weight * dout, activations, cotangent, weight, momentum, right_factor
     )
     step_scale = (dout / rank) ** 0.5
-    momentum_next, weight_step, right_next = output_call(
-        step_scale, buffer, orthonormal.reshape(rows, rank), right_high, right_low, right_turned, scale
+    momentum_next, weight_step, right_next, input_grad = output_call(
+        step_scale, buffer, orthonormal.reshape(rows, rank), right_high, right_low, right_turned, scale, input_sums
     )
     return input_grad, momentum_next, right_next, weight_step
 

time: 113 us -> 109 us (0.965)
  Pallas kernels: 111 us -> 109 us
    pallas_call x1, Pallas kernels: 15.9 us -> 13.8 us  [output_call(): pl.pallas_call(functools.partial(output_kernel, step_scale), grid=(steps,...]
where the time goes in v4:
time: 109 us
  Pallas kernels  109 us (100%)
    pallas_call x1, Pallas kernels, factor_call(): pl.pallas_call(functools.partial(factor_kernel, n_row, n_col, ridge), out...  94.7 us
    pallas_call x1, Pallas kernels, output_call(): pl.pallas_call(functools.partial(output_kernel, step_scale), grid=(steps,...  13.8 us

profile of v4, /device:TPU:0, one launch (start us, length us, event | category | flops | bytes accessed | tf_op | source)
XLA Modules:
  0.0 109.2 jit_solution(2483988889427850075)
XLA Ops:
  0.6 94.7 %factors.1 = (bf16[16,1152]{1,0:T(8,128)(2,1)}, f32[2304,1152]{1,0:T(8,128)}, f32[8,288,256]{2,1,0:T(8,128)}, bf16[256,1152]{1,0:T(8,128)(2,1)}, bf16[256,1152]{...) custom-call(bf16[16,1152]{1,0:T(8,128)(2,1)} %act_ref.1, bf16[8,2304]{1,0:T(8,128)(2,1)} %cot_ref.1, ...), custom_call_target="tpu_custom_call" | custom-call | tf_op jit(solution)/shard_map/factors/pallas_call | solution.py:850
  95.4 13.8 %outputs.1 = (f32[2304,1152]{1,0:T(8,128)}, bf16[2304,1152]{1,0:T(8,128)(2,1)}, f32[1152,256]{1,0:T(8,128)}, bf16[16,1152]{1,0:T(8,128)(2,1)}) custom-call(f32[2304,1152]{1,0:T(8,128)} %get-tuple-element.15.buffer_ref, f32[2304,256]{1,0:T(8,128)} %bitcast.1, bf16[256,1152]{1,0:T(8,128)(2,1)} %get-tuple-element.17.right_high_ref, ...), custom_call_target="tpu_custom_call" | custom-call | tf_op jit(solution)/shard_map/outputs/pallas_call | solution.py:970

commit v5 on v4

--- a/solution.py
+++ b/solution.py
@@ -708,15 +708,25 @@
 
     absorb(0, col)
     settle(1)
-    forward(0, outer - 2)
+
+    @pl.when(near > 0)
+    def _():
+        forward(0, outer - 2)
+
 
     def absorb_first(n, carry):
         absorb_outer(0, n)
         return carry
 
-    lax.fori_loop(0, outer - 1, absorb_first, 0)
+    lax.fori_loop(0, outer - 2, absorb_first, 0)
     absorb_inner(0, me_out)
     absorb(1, col)
+
+    @pl.when(near == 0)
+    def _():
+        forward(0, outer - 2)
+
+    absorb_outer(0, outer - 2)
 
     def absorb_second(n, carry):
         forward(1, n)
@@ -733,13 +743,14 @@
     proj_sums[0].cross()
     forward(1, outer - 2)
     absorb_outer(1, outer - 2)
+    absorb_inner(1, arrival(0))
     gram_sums[0].spread()
 
     def absorb_third(n, carry):
         absorb_inner(1, arrival(n))
         return carry
 
-    lax.fori_loop(0, outer - 1, absorb_third, 0)
+    lax.fori_loop(1, outer - 1, absorb_third, 0)
     gram_sums[1].begin()
     proj_sums[1].begin()
     gram_sums[0].end()
@@ -750,7 +761,7 @@
         invert_block(low, block, work, corner, diagonal)
         if low == 0:
             gram_sums[1].spread()
-    proj_sums[0].spread()
+            proj_sums[0].spread()
     finish_half(0, rest)
     proj_sums[0].end()
     right_turned_parts = [right_half(0)]

time: 109 us -> 107 us (0.982)
  Pallas kernels: 109 us -> 106 us
    pallas_call x1, Pallas kernels: 94.7 us -> 92 us  [factor_call(): pl.pallas_call(functools.partial(factor_kernel, n_row, n_col, ridge), out...]
where the time goes in v5:
time: 107 us
  Pallas kernels  106 us (99%)
    pallas_call x1, Pallas kernels, factor_call(): pl.pallas_call(functools.partial(factor_kernel, n_row, n_col, ridge), out...  92 us
    pallas_call x1, Pallas kernels, output_call(): pl.pallas_call(functools.partial(output_kernel, step_scale), grid=(steps,...  13.8 us

profile of v5, /device:TPU:0, one launch (start us, length us, event | category | flops | bytes accessed | tf_op | source)
XLA Modules:
  0.0 106.5 jit_solution(15486692043602990629)
XLA Ops:
  0.6 92.0 %factors.1 = (bf16[16,1152]{1,0:T(8,128)(2,1)}, f32[2304,1152]{1,0:T(8,128)}, f32[8,288,256]{2,1,0:T(8,128)}, bf16[256,1152]{1,0:T(8,128)(2,1)}, bf16[256,1152]{...) custom-call(bf16[16,1152]{1,0:T(8,128)(2,1)} %act_ref.1, bf16[8,2304]{1,0:T(8,128)(2,1)} %cot_ref.1, ...), custom_call_target="tpu_custom_call" | custom-call | tf_op jit(solution)/shard_map/factors/pallas_call | solution.py:861
  92.7 13.8 %outputs.1 = (f32[2304,1152]{1,0:T(8,128)}, bf16[2304,1152]{1,0:T(8,128)(2,1)}, f32[1152,256]{1,0:T(8,128)}, bf16[16,1152]{1,0:T(8,128)(2,1)}) custom-call(f32[2304,1152]{1,0:T(8,128)} %get-tuple-element.15.buffer_ref, f32[2304,256]{1,0:T(8,128)} %bitcast.1, bf16[256,1152]{1,0:T(8,128)(2,1)} %get-tuple-element.17.right_high_ref, ...), custom_call_target="tpu_custom_call" | custom-call | tf_op jit(solution)/shard_map/outputs/pallas_call | solution.py:981

commit v6 on v5

--- a/solution.py
+++ b/solution.py
@@ -521,7 +521,10 @@
 
     def forward(h, n):
         q = arrival(n)
-        gather_outer(h, q, 0).wait_recv()
+        piece_ref = left_ref.at[h, q * inner + me_in]
+        remote(
+            piece_ref, piece_ref, gather_send_sem.at[h, 0, q], gather_outer_sem.at[h, q], (row, col)
+        ).wait_recv()
         onward(h, q, True)
         for d in range(inner - 1):
             gather_inner(h, d, q).start()

time: 107 us -> 107 us (level)
  no operation moved by 1% of the time
where the time goes in v6:
time: 107 us
  Pallas kernels  106 us (99%)
    pallas_call x1, Pallas kernels, factor_call(): pl.pallas_call(functools.partial(factor_kernel, n_row, n_col, ridge), out...  92 us
    pallas_call x1, Pallas kernels, output_call(): pl.pallas_call(functools.partial(output_kernel, step_scale), grid=(steps,...  13.8 us

profile of v6, /device:TPU:0, one launch (start us, length us, event | category | flops | bytes accessed | tf_op | source)
XLA Modules:
  0.0 106.5 jit_solution(15486692043602990629)
XLA Ops:
  0.6 92.0 %factors.1 = (bf16[16,1152]{1,0:T(8,128)(2,1)}, f32[2304,1152]{1,0:T(8,128)}, f32[8,288,256]{2,1,0:T(8,128)}, bf16[256,1152]{1,0:T(8,128)(2,1)}, bf16[256,1152]{...) custom-call(bf16[16,1152]{1,0:T(8,128)(2,1)} %act_ref.1, bf16[8,2304]{1,0:T(8,128)(2,1)} %cot_ref.1, ...), custom_call_target="tpu_custom_call" | custom-call | tf_op jit(solution)/shard_map/factors/pallas_call | solution.py:864
  92.7 13.8 %outputs.1 = (f32[2304,1152]{1,0:T(8,128)}, bf16[2304,1152]{1,0:T(8,128)(2,1)}, f32[1152,256]{1,0:T(8,128)}, bf16[16,1152]{1,0:T(8,128)(2,1)}) custom-call(f32[2304,1152]{1,0:T(8,128)} %get-tuple-element.15.buffer_ref, f32[2304,256]{1,0:T(8,128)} %bitcast.1, bf16[256,1152]{1,0:T(8,128)(2,1)} %get-tuple-element.17.right_high_ref, ...), custom_call_target="tpu_custom_call" | custom-call | tf_op jit(solution)/shard_map/outputs/pallas_call | solution.py:984
